TPU v7x, 128 devices: a whole 4x4x4 slice. The times are simulated.
128 devices in a mesh: head: 2 (over y_hi), block: 2 (over y_lo), tok: 32 (over z, x, core).
Axes of the slice: x: 4, y: 4 (y_hi: 2, y_lo: 2; y = y_hi * 2 + y_lo), z: 4, core: 2. Of those that a mesh axis runs over, the one named last changes fastest.
Arguments:
- tokens: bfloat16 [2, 16384, 2048], P('block', 'tok'), may hold values from -6 to 6
- input_weight: bfloat16 [2048, 3, 2048], P(None, None, 'head'), may hold values from -0.125 to 0.125
- rate_weight: bfloat16 [2048, 4], P(None, 'head'), may hold values from -0.375 to 0.375
- fast_init: bfloat16 [4, 3, 512, 512], P('head'), may hold values from -0.25 to 0.25
- output_weight: bfloat16 [2048, 2048], P('head'), may hold values from -0.125 to 0.125
Outputs:
- mixed: bfloat16 [2, 16384, 2048], P('block', 'tok', 'head')
All inputs are finite; a program needn't handle non-finite values.
Results may differ from a plain program's by a relative error of at most 0.005.
Values sent between devices are 32-bit elements; how exact they have to be, the bound alone decides.
A program may use at most 128 MiB of HBM per device.

v0:
```python
import jax
import jax.numpy as jnp
from jax import lax
from jax.sharding import PartitionSpec as P

epsilon = 1e-06
step_size = 0.03
highest = lax.Precision.HIGHEST


def passed_along(block, axis, distance):
    devices = range(lax.axis_size(axis))
    route = [(i - distance, i) for i in devices if i - distance in devices]
    return lax.ppermute(block, axis, route)


def matmul(left, right):
    return jnp.dot(left, right, precision=highest, preferred_element_type=jnp.float32)


def normalize(values):
    return values / jnp.sqrt(jnp.mean(values * values, axis=-1, keepdims=True) + epsilon)


def fast_grad(weights, keys, targets):
    gate = matmul(keys, weights[0])
    upper = matmul(keys, weights[1])
    sigma = jax.nn.sigmoid(gate)
    active = gate * sigma
    hidden = active * upper
    grad_down = matmul(targets.T, hidden)
    back = matmul(targets, weights[2])
    grad_upper = matmul(keys.T, back * active)
    grad_gate = matmul(keys.T, back * upper * sigma * (1.0 + gate * (1.0 - sigma)))
    return jnp.stack([grad_gate, grad_upper, grad_down])


def fast_apply(weights, queries):
    gate = matmul(queries, weights[0])
    upper = matmul(queries, weights[1])
    hidden = gate * jax.nn.sigmoid(gate) * upper
    return normalize(matmul(hidden, weights[2].T))


def body(tokens, input_weight, rate_weight, fast_init, output_weight):
    block_count, tok_rows, model_width = tokens.shape
    head_count, _, head_dim, fast_dim = fast_init.shape
    start_weights = fast_init.astype(jnp.float32)
    flattened = tokens.reshape(block_count * tok_rows, model_width)
    projected = jnp.dot(
        flattened, input_weight.reshape(model_width, -1), preferred_element_type=jnp.float32
    )
    projected = projected.reshape(block_count, tok_rows, 3, head_count, head_dim)
    rates = jax.nn.softplus(jnp.dot(flattened, rate_weight, preferred_element_type=jnp.float32))
    rates = rates.reshape(block_count, tok_rows, head_count)
    queries = normalize(projected[:, :, 0])
    keys = normalize(projected[:, :, 1])
    targets = projected[:, :, 2] * rates[:, :, :, None]
    base_rms = jnp.sqrt(jnp.mean(start_weights * start_weights, axis=2, keepdims=True))
    head_grads = jax.vmap(fast_grad, in_axes=(0, 1, 1))
    position = lax.axis_index("block")
    groups = lax.axis_size("block")
    chosen = [start_weights]
    incoming = start_weights
    for section in range(groups):
        weights = incoming
        local = 0
        partial_value = head_grads(weights, keys[local], targets[local])
        pieces = lax.psum_scatter(partial_value, "tok", scatter_dimension=3, tiled=True)
        width = pieces.shape[3]
        squares = jnp.sum(pieces * pieces, axis=(2, 3))
        total_sq = lax.psum(squares, "tok")
        scale = jnp.sqrt(total_sq / (head_dim * fast_dim) + epsilon)[:, :, None, None]
        start = lax.axis_index("tok") * width
        own_weights = lax.dynamic_slice_in_dim(weights, start, width, 3)
        own_rms = lax.dynamic_slice_in_dim(base_rms, start, width, 3)
        moved = own_weights + step_size * pieces / scale
        fresh = moved * own_rms / jnp.sqrt(jnp.mean(moved * moved, axis=2, keepdims=True) + epsilon)
        weights = lax.all_gather(fresh, "tok", axis=3, tiled=True)
        chosen[local] = jnp.where(position == section, weights, chosen[local])
        if section + 1 < groups:
            incoming = passed_along(weights, "block", 1)
    head_apply = jax.vmap(fast_apply, in_axes=(0, 1), out_axes=1)
    joined = []
    local = 0
    applied = head_apply(chosen[local], queries[local])
    joined.append(applied.reshape(tok_rows, head_count * head_dim))
    joined = (
        jnp.stack(joined)
        .reshape(block_count * tok_rows, head_count * head_dim)
        .astype(jnp.bfloat16)
    )
    partial_out = jnp.dot(joined, output_weight, preferred_element_type=jnp.float32)
    partial_out = partial_out.reshape(block_count, tok_rows, model_width)
    return lax.psum_scatter(partial_out, "head", scatter_dimension=2, tiled=True).astype(
        jnp.bfloat16
    )


def solution(mesh):
    placed = (
        P("block", "tok", None),
        P(None, None, "head"),
        P(None, "head"),
        P("head", None, None, None),
        P("head", None),
    )
    return jax.shard_map(
        body, mesh=mesh, in_specs=placed, out_specs=P("block", "tok", "head"), check_vma=False
    )
```

profile of v0, /device:TPU:8, one launch (start us, length us, event | category | flops | bytes accessed | tf_op | source)
XLA Modules:
  0.0 827.7 jit_solution(6733005602457865795)
XLA Ops:
  6.5 17.1 %copy.79 = bf16[2048,3,1024]{0,2,1:T(8,128)(2,1)} copy(bf16[2048,3,1024]{2,0,1:T(8,128)(2,1)} %param.6) | data formatting | bytes 25165824 | tf_op args[1]
  23.6 9.5 %convolution_bitcast_fusion.1 = f32[1,512,3,2,512]{1,4,3,2,0:T(8,128)S(1)} fusion(bf16[3,2,512,2048]{3,2,1,0:T(8,128)(2,1)} %bitcast.143, bf16[1,512,2048]{2,1,0:T(8,128)(2,1)S(1)} %copy-done), kind=kOutput, calls=%fused_computation.5 | convolution fusion | flops 6442450944 | bytes 20971520 | tf_op jit(solution)/shard_map/dot_general | solution.py:50
  33.7 3.6 copy-done.4
  43.6 4.0 fusion.52
  47.5 4.5 fusion.47
  52.0 4.0 fusion.67
  56.0 3.3 maximum_bitcast_fusion
  59.3 10.3 %copy.87 = f32[2,3,512,512]{2,0,1,3:T(2,128)} copy(f32[2,3,512,512]{3,2,0,1:T(8,128)} %maximum_bitcast_fusion) | data formatting | bytes 12582912 | tf_op jit(solution)/shard_map/vmap()/transpose | solution.py:68
  69.7 3.2 copy.80
  73.0 3.5 convert_element_type.12
  78.4 109.4 %all-reduce.5.cloned.1.call-done = f32[2,3,512,512]{2,0,1,3:T(2,128)} async-done(((f32[2,3,512,512]{2,0,1,3:T(2,128)}), f32[2,3,512,512]{2,0,1,3:T(2,128)}) %all-reduce.5.cloned.1.call-update) | async-done | bytes 6291472
  189.0 66.2 %psum.14 = f32[2,3]{0,1:T(4,128)S(1)} all-reduce(f32[2,3]{0,1:T(4,128)S(1)} %get-tuple-element.9), channel_id=1, replica_groups=mesh['head'=2,'block'=2,'tok'=32] {'tok'}, use_global_device_ids=true, to_apply=%region_4.5 | all-reduce | flops 6 | bytes 48 | tf_op jit(solution)/shard_map/psum | solution.py:72
  258.3 45.5 %all-gather.3.cloned.1.call-done = f32[2,3,512,512]{2,0,1,3:T(2,128)} async-done(((f32[2,3,512,16]{2,0,1,3:T(2,128)}), f32[2,3,512,512]{2,0,1,3:T(2,128)}) %all-gather.3.cloned.1.call-update) | async-done | bytes 6291472 | tf_op jit(solution)/shard_map/all_gather | solution.py:79
  303.8 4.0 copy.91
  309.5 137.8 %collective-permute-done = f32[2,3,512,512]{2,3,1,0:T(8,128)S(1)} collective-permute-done((f32[2,3,512,512]{2,3,1,0:T(8,128)S(1)}, f32[2,3,512,512]{2,3,1,0:T(8,128)S(1)}, u32[]{:S(2)}, u32[]{:S(2)}) %collective-permute-start) | collective-permute-done | bytes 6291488 | tf_op jit(solution)/shard_map/ppermute | solution.py:14
  447.4 10.1 %fusion.5 = f32[2,512,512]{2,1,0:T(8,128)S(1)} fusion(f32[2,3,512,512]{2,3,1,0:T(8,128)S(1)} %collective-permute-done, f32[1,512,3,2,512]{1,4,3,2,0:T(8,128)} %copy-done.2, f32[512,2]{0,1:T(2,128)S(1)} %compare_select_fusion), kind=kOutput, calls=%fused_computation.17 | convolution fusion | flops 3221749760 | bytes 6295552 | tf_op jit(solution)/shard_map/vmap()/dot_general | solution.py:18
  457.5 8.7 %fusion.3 = f32[2,512,512]{2,1,0:T(8,128)S(1)} fusion(f32[2,3,512,512]{2,3,1,0:T(8,128)S(1)} %collective-permute-done, f32[1,512,3,2,512]{1,4,3,2,0:T(8,128)} %copy-done.2, f32[512,2]{0,1:T(2,128)S(1)} %add_sqrt_fusion.2), kind=kOutput, calls=%fused_computation.13 | convolution fusion | flops 3221749760 | bytes 6295552 | tf_op jit(solution)/shard_map/vmap()/dot_general | solution.py:18
  466.2 4.0 fusion.62
  470.2 6.8 fusion.4
  476.9 4.5 fusion.57
  481.4 4.0 fusion.72
  485.4 3.4 maximum_bitcast_fusion.1
  488.8 10.3 %copy.98 = f32[2,3,512,512]{2,0,1,3:T(2,128)} copy(f32[2,3,512,512]{3,2,0,1:T(8,128)} %maximum_bitcast_fusion.1) | data formatting | bytes 12582912 | tf_op jit(solution)/shard_map/vmap()/transpose | solution.py:68
  499.2 114.3 %all-reduce.7.cloned.1.call-done = f32[2,3,512,512]{2,0,1,3:T(2,128)} async-done(((f32[2,3,512,512]{2,0,1,3:T(2,128)}), f32[2,3,512,512]{2,0,1,3:T(2,128)}) %all-reduce.7.cloned.1.call-update) | async-done | bytes 6291472
  614.7 66.2 %psum.15 = f32[2,3]{0,1:T(4,128)S(1)} all-reduce(f32[2,3]{0,1:T(4,128)S(1)} %get-tuple-element.7), channel_id=1, replica_groups=mesh['head'=2,'block'=2,'tok'=32] {'tok'}, use_global_device_ids=true, to_apply=%region_9.10 | all-reduce | flops 6 | bytes 48 | tf_op jit(solution)/shard_map/psum | solution.py:72
  684.5 45.0 %all-gather.5.cloned.1.call-done = f32[2,3,512,512]{2,0,1,3:T(2,128)} async-done(((f32[2,3,512,16]{2,0,1,3:T(2,128)}), f32[2,3,512,512]{2,0,1,3:T(2,128)}) %all-gather.5.cloned.1.call-update) | async-done | bytes 6291472 | tf_op jit(solution)/shard_map/all_gather | solution.py:79
  729.5 6.8 copy_select_fusion
  736.3 8.3 %fusion.2 = f32[2,512,512]{2,1,0:T(8,128)S(1)} fusion(f32[2,3,512,512]{2,3,1,0:T(8,128)S(1)} %copy_select_fusion, f32[1,512,3,2,512]{1,4,3,2,0:T(8,128)} %copy-done.2, f32[512,2]{0,1:T(2,128)S(1)} %add_sqrt_fusion.3), kind=kOutput, calls=%fused_computation.11 | convolution fusion | flops 3221749760 | bytes 6295552 | tf_op jit(solution)/shard_map/vmap()/dot_general | solution.py:18
  744.7 8.5 %fusion.1 = f32[2,512,512]{2,1,0:T(8,128)S(1)} fusion(f32[2,3,512,512]{2,3,1,0:T(8,128)S(1)} %copy_select_fusion, f32[1,512,3,2,512]{1,4,3,2,0:T(8,128)} %copy-done.2, f32[512,2]{0,1:T(2,128)S(1)} %add_sqrt_fusion.3), kind=kOutput, calls=%fused_computation.9 | convolution fusion | flops 3221749760 | bytes 6295552 | tf_op jit(solution)/shard_map/vmap()/dot_general | solution.py:18
  753.2 4.0 multiply_reduce_fusion.1
  757.5 4.3 convolution_bitcast_fusion
  761.8 56.4 %reduce-scatter.2.cloned.1.call-done = f32[1,512,1024]{2,1,0:T(8,128)} async-done(((f32[1,512,2048]{2,1,0:T(8,128)}), f32[1,512,1024]{2,1,0:T(8,128)}) %reduce-scatter.2.cloned.1.call-update) | async-done | bytes 2097168 | tf_op jit(solution)/shard_map/reduce_scatter | solution.py:95
  (58 shorter events, 22.0 us)
Async XLA Ops:
  6.5 17.1 %copy-start = (bf16[1,512,2048]{2,1,0:T(8,128)(2,1)S(1)}, bf16[1,512,2048]{2,1,0:T(8,128)(2,1)}, u32[]{:S(2)}) copy-start(bf16[1,512,2048]{2,1,0:T(8,128)(2,1)} %param.5) | copy-start | bytes 6291460
  6.5 181.3 %all-reduce.5.cloned.1.call-start = ((), (), s32[]{:S(2)}) async-start(), calls=%async_computation.4 | async-start | bytes 12582912
  33.1 18.9 %copy-start.2 = (f32[1,512,3,2,512]{1,4,3,2,0:T(8,128)}, f32[1,512,3,2,512]{1,4,3,2,0:T(8,128)S(1)}, u32[]{:S(2)}) copy-start(f32[1,512,3,2,512]{1,4,3,2,0:T(8,128)S(1)} %convolution_bitcast_fusion.1) | copy-start | bytes 18874372
  33.1 4.2 copy-start.4
  39.2 1.9 copy-start.6
  69.7 234.1 %all-gather.3.cloned.1.call-start = ((), (), s32[]{:S(2)}) async-start(), calls=%async_computation.1 | async-start | bytes 6488064 | tf_op jit(solution)/shard_map/all_gather | solution.py:79
  72.9 3.5 copy-start.7
  258.3 355.2 %all-reduce.7.cloned.1.call-start = ((), (), s32[]{:S(2)}) async-start(), calls=%async_computation.5 | async-start | bytes 12582912
  307.8 139.5 %collective-permute-start = (f32[2,3,512,512]{2,3,1,0:T(8,128)S(1)}, f32[2,3,512,512]{2,3,1,0:T(8,128)S(1)}, u32[]{:S(2)}, u32[]{:S(2)}) collective-permute-start(f32[2,3,512,512]{2,3,1,0:T(8,128)S(1)} %copy.91), channel_id=1, source_target_pairs={{0,32},{1,33},{2,34},{3,35},{4,36},{5,37},{6,38},{7,39},{8,40},{9,... | collective-permute-start | bytes 18874376 | tf_op jit(solution)/shard_map/ppermute | solution.py:14
  447.4 22.8 %copy-start.5 = (f32[2,3,512,512]{2,3,1,0:T(8,128)}, f32[2,3,512,512]{2,3,1,0:T(8,128)S(1)}, u32[]{:S(2)}) copy-start(f32[2,3,512,512]{2,3,1,0:T(8,128)S(1)} %collective-permute-done) | copy-start | bytes 18874372
  447.4 18.8 %slice-start = ((s8[6291456]{0:T(1024)(128)(4,1)}), s8[4194304]{0:T(1024)(128)(4,1)S(1)}, s32[]{:S(2)}) async-start(s8[6291456]{0:T(1024)(128)(4,1)} %bitcast.144), calls=%async_computation.6 | async-start | bytes 8388608
  457.5 8.7 %slice-start.1 = ((s8[6291456]{0:T(1024)(128)(4,1)}), s8[2097152]{0:T(1024)(128)(4,1)S(1)}, s32[]{:S(2)}) async-start(s8[6291456]{0:T(1024)(128)(4,1)} %bitcast.144), calls=%async_computation.7 | async-start | bytes 4194304
  499.2 230.3 %all-gather.5.cloned.1.call-start = ((), (), s32[]{:S(2)}) async-start(), calls=%async_computation.2 | async-start | bytes 6488064 | tf_op jit(solution)/shard_map/all_gather | solution.py:79
  684.0 134.2 %reduce-scatter.2.cloned.1.call-start = ((), (), s32[]{:S(2)}) async-start(), calls=%async_computation.3 | async-start | bytes 6291456 | tf_op jit(solution)/shard_map/reduce_scatter | solution.py:95
  753.2 4.3 copy-start.3
  761.8 59.1 %copy-start.1 = (bf16[1,512,2048]{2,1,0:T(8,128)(2,1)S(1)}, bf16[1,512,2048]{2,1,0:T(8,128)(2,1)}, u32[]{:S(2)}) copy-start(bf16[1,512,2048]{2,1,0:T(8,128)(2,1)} %param.5) | copy-start | bytes 6291460
Sparse Core Ops, SparseCore 0:
  69.8 117.9 all-reduce.4
  258.4 45.3 all-gather.2
  499.3 114.1 all-reduce.6
  684.1 45.3 all-gather.4
  762.0 56.2 reduce-scatter.1
where the time goes:
time: 833 us; the launch traced here: 828 us
  waiting for transfers between devices  508 us (61%)
  blocking collectives  132 us (16%)
  matrix products  91.1 us (11%)
  local copies, waits for them, and re-layouts  51 us (6%)
  other arithmetic  28.1 us (3%)
  between operations  14.3 us (2%)
    unnamed x7, waiting for transfers between devices  224 us
    ppermute x1, waiting for transfers between devices, passed_along(): return lax.ppermute(block, axis, route)  138 us
    psum x2, blocking collectives, body(): total_sq = lax.psum(squares, 'tok')  132 us
    all_gather x2, waiting for transfers between devices, body(): weights = lax.all_gather(fresh, 'tok', axis=3, tiled=True)  90.5 us
    dot_general x15, matrix products, matmul(): jnp.dot(left, right, precision=highest, preferred_element_type=jnp.float32)  76.7 us
    reduce_scatter x1, waiting for transfers between devices, body(): lax.psum_scatter(partial_out, 'head', scatter_dimension=2, tiled=True)  56.4 us
    unnamed x23, local copies, waits for them, and re-layouts  24.5 us
    transpose x2, local copies, waits for them, and re-layouts, body(): partial_value = head_grads(weights, keys[local], targets[local])  20.6 us
  transfers between devices with their start and end apart: 6, of which 6 were waited for; matrix products, arithmetic and copies ran while one was open for 1% of the time, Pallas kernels for 0%

commit v1 on v0

v1 whole, which is shorter than its diff:
```python
import jax
import jax.numpy as jnp
from jax import lax
from jax.experimental import pallas as pl
from jax.experimental.pallas import tpu as pltpu
from jax.sharding import PartitionSpec as P

epsilon = 1e-06
step_size = 0.03
MESH = pl.DeviceIdType.MESH
f32 = jnp.float32
bf16 = jnp.bfloat16
N = 512
ORDER = (1, 0, 2)


def split(x):
    hi = x.astype(bf16)
    return hi, (x - hi.astype(f32)).astype(bf16)


def dot(a, b):
    return jnp.dot(a, b, preferred_element_type=f32)


def mm3(ah, al, bh, bl):
    return dot(ah, bh) + (dot(ah, bl) + dot(al, bh))


def dot_nt(a, b):
    return lax.dot_general(a, b, (((1,), (1,)), ((), ())), preferred_element_type=f32)


def mm3_nt(ah, al, bh, bl):
    return dot_nt(ah, bh) + (dot_nt(ah, bl) + dot_nt(al, bh))


def normalize(v):
    return v * (1.0 / jnp.sqrt(jnp.mean(v * v, axis=-1, keepdims=True) + epsilon))


def chain_kernel(
    k_ref, y_ref, q_ref, w0_ref, o_ref,
    k_got, y_got, q_got, o_mine, o_got,
    kh, kl, kth, ktl, yh, yl, yth, ytl,
    hh, hl, p3h, p3l, p1h, p1l,
    w, wh, wl, r0, gp, gf, gf1, r1, r2,
    rs_s, rs_r, ag_s, ag_r, a1_s, a1_r, sh_s, sh_r, ex_s, ex_r,
):
    tok = lax.axis_index("tok")
    block = lax.axis_index("block")
    core = lax.rem(tok, 2)
    chip = lax.div(tok, 2)
    x = lax.rem(chip, 4)
    z = lax.div(chip, 4)

    def at_x(d):
        return {"tok": (z * 4 + lax.rem(x + d + 4, 4)) * 2 + core}

    def at_z(d):
        return {"tok": (lax.rem(z + d + 4, 4) * 4 + x) * 2 + core}

    partner = {"tok": chip * 2 + (1 - core)}
    other_block = {"block": 1 - block}

    barrier = pltpu.get_barrier_semaphore()
    everyone = (partner, at_x(1), at_x(-1), at_z(1), at_z(-1), other_block)
    for device in everyone:
        pl.semaphore_signal(barrier, inc=1, device_id=device, device_id_type=MESH)
    pl.semaphore_wait(barrier, len(everyone))

    def rcopy(src, dst, ss, rs, device):
        return pltpu.make_async_remote_copy(
            src_ref=src, dst_ref=dst, send_sem=ss, recv_sem=rs,
            device_id=device, device_id_type=MESH,
        )

    mine = pl.ds(pl.multiple_of(core * N, N), N)
    theirs = pl.ds(pl.multiple_of((1 - core) * N, N), N)
    swaps = [
        rcopy(src.at[:, theirs], dst, ex_s.at[n], ex_r.at[n], partner)
        for n, (src, dst) in enumerate(((k_ref, k_got), (y_ref, y_got), (q_ref, q_got)))
    ]
    for copy in swaps:
        copy.start()

    for m in range(3):
        start = w0_ref[core, m].astype(f32)
        w[m] = start
        wh[m], wl[m] = split(start)
        r0[m] = jnp.sqrt(jnp.mean(start * start, axis=0, keepdims=True))

    def prepare(load, base, scale, h_ref, l_ref, th_ref, tl_ref):
        @pl.loop(0, 2)
        def _(i):
            rows = pl.ds(pl.multiple_of(i * 256, 256), 256)
            v = load(rows)
            if scale:
                v = normalize(v)
            hi, lo = split(v)
            to = pl.ds(pl.multiple_of(base + i * 256, 256), 256)
            h_ref[to, :] = hi
            l_ref[to, :] = lo
            th_ref[:, to] = hi.T
            tl_ref[:, to] = lo.T

    prepare(lambda r: k_ref[r, mine], 0, True, kh, kl, kth, ktl)
    prepare(lambda r: y_ref[r, mine], 0, False, yh, yl, yth, ytl)
    swaps[0].wait_recv()
    prepare(lambda r: k_got[r, :], N, True, kh, kl, kth, ktl)
    swaps[1].wait_recv()
    prepare(lambda r: y_got[r, :], N, False, yh, yl, yth, ytl)
    swaps[2].wait_recv()

    def rows_of(s, j1, j2=None, off=0, count=64):
        at = s * 256 + j1 * 64 + off
        if j2 is not None:
            at = at + j2 * 16
        return pl.ds(pl.multiple_of(at, 8), count)

    def reduce_stage(m, piece, n, got, store, i, go, ss, rs):
        src = gp.at[m]
        nxt, prv, far = lax.rem(i + 1, 4), lax.rem(i + 3, 4), lax.rem(i + 2, 4)
        right, left = go(1), go(-1)
        c0 = rcopy(src.at[piece(far, 0, n)], got.at[0], ss.at[0], rs.at[0], right)
        c1 = rcopy(src.at[piece(far, n, n)], got.at[1], ss.at[1], rs.at[1], left)
        c2 = rcopy(src.at[piece(nxt, n, n)], got.at[2], ss.at[2], rs.at[2], right)
        c3 = rcopy(src.at[piece(prv, 0, n)], got.at[3], ss.at[3], rs.at[3], left)
        for c in (c0, c1, c2, c3):
            c.start()
        yield
        c0.wait_recv()
        got[0] = got[0] + gp[m, piece(nxt, 0, n), :]
        c4 = rcopy(got.at[0], got.at[4], ss.at[4], rs.at[4], right)
        c4.start()
        c1.wait_recv()
        got[1] = got[1] + gp[m, piece(prv, n, n), :]
        c5 = rcopy(got.at[1], got.at[5], ss.at[5], rs.at[5], left)
        c5.start()
        yield
        for c in (c2, c3, c4, c5):
            c.wait_recv()
        store(0, gp[m, piece(i, 0, n), :] + got[3] + got[4])
        store(n, gp[m, piece(i, n, n), :] + got[2] + got[5])
        sent.extend((c0, c1, c2, c3, c4, c5))

    def gather_stage(buf, piece, n, i, go, ss, rs, done):
        nxt, prv, far = lax.rem(i + 1, 4), lax.rem(i + 3, 4), lax.rem(i + 2, 4)
        right, left = go(1), go(-1)

        def send(k, rows, device):
            return rcopy(buf.at[rows], buf.at[rows], ss.at[k], rs.at[k], device)

        c0 = send(0, piece(i, 0, 2 * n), right)
        c1 = send(1, piece(i, 0, 2 * n), left)
        c0.start()
        c1.start()
        yield
        send(0, piece(prv, 0, 2 * n), right).wait_recv()
        c2 = send(2, piece(prv, 0, n), right)
        c2.start()
        send(1, piece(nxt, 0, 2 * n), left).wait_recv()
        c3 = send(3, piece(nxt, n, n), left)
        c3.start()
        yield
        send(2, piece(far, 0, n), right).wait_recv()
        send(3, piece(far, n, n), left).wait_recv()
        done.extend((c0, c1, c2, c3))

    axes = ((x, at_x, z, at_z), (z, at_z, x, at_x))

    def gather(buf, m, s, ss, rs, done):
        i1, go1, i2, go2 = axes[s]
        yield from gather_stage(
            buf.at[m], lambda j, o, c: rows_of(s, i1, j, o, c), 8, i2, go2,
            ss.at[m, s, 0], rs.at[m, s, 0], done,
        )
        yield from gather_stage(
            buf.at[m], lambda j, o, c: rows_of(s, j, None, o, c), 32, i1, go1,
            ss.at[m, s, 1], rs.at[m, s, 1], done,
        )

    def shard(m, s):
        i1, _, i2, _ = axes[s]
        rows = rows_of(s, i1, i2, 0, 16)
        return rcopy(gf.at[m, rows], gf1.at[m, rows], sh_s.at[m, s], sh_r.at[m, s], other_block)

    sent = []

    def whole(m, s):
        i1, go1, i2, go2 = axes[s]

        def store1(o, v):
            gp[m, rows_of(s, i1, None, o, 32), :] = v

        def store2(o, v):
            gf[m, rows_of(s, i1, i2, o, 8), :] = v

        yield from reduce_stage(
            m, lambda j, o, c: rows_of(s, j, None, o, c), 32, r1.at[m, s], store1, i1, go1,
            rs_s.at[m, s, 0], rs_r.at[m, s, 0],
        )
        yield from reduce_stage(
            m, lambda j, o, c: rows_of(s, i1, j, o, c), 8, r2.at[m, s], store2, i2, go2,
            rs_s.at[m, s, 1], rs_r.at[m, s, 1],
        )

        @pl.when(block == 0)
        def _():
            shard(m, s).start()

        yield from gather(gf, m, s, ag_s, ag_r, sent)

    def update(m, g_ref):
        g = g_ref[m]
        total = jnp.sum(jnp.sum(g * g, axis=0, keepdims=True), axis=1, keepdims=True)
        scale = step_size / jnp.sqrt(total / (N * N) + epsilon)
        moved = w[m] + g * scale
        column = jnp.mean(moved * moved, axis=0, keepdims=True)
        fresh = moved * (r0[m] / jnp.sqrt(column + epsilon))
        w[m] = fresh
        wh[m], wl[m] = split(fresh)

    def drive(streams, finish):
        left = {m: list(streams[m]) for m in streams}
        while left:
            for m in [m for m in ORDER if m in left]:
                still = []
                for g in left[m]:
                    try:
                        next(g)
                        still.append(g)
                    except StopIteration:
                        pass
                left[m] = still
                if not still:
                    del left[m]
                    finish(m)

    @pl.when(block == 1)
    def _():
        done = []

        def first(m, s):
            shard(m, s).wait_recv()
            yield from gather(gf1, m, s, a1_s, a1_r, done)

        drive({m: [first(m, s) for s in range(2)] for m in range(3)}, lambda m: update(m, gf1))
        for c in done:
            c.wait_send()

    @pl.loop(0, 4)
    def _(i):
        rows = pl.ds(pl.multiple_of(i * 256, 256), 256)
        ah, al = kh[rows, :], kl[rows, :]
        gate = mm3(ah, al, wh[0], wl[0])
        upper = mm3(ah, al, wh[1], wl[1])
        back = mm3(yh[rows, :], yl[rows, :], wh[2], wl[2])
        sigma = jax.nn.sigmoid(gate)
        active = gate * sigma
        hh[rows, :], hl[rows, :] = split(active * upper)
        p3h[rows, :], p3l[rows, :] = split(back * active)
        p1h[rows, :], p1l[rows, :] = split(back * upper * sigma * (1.0 + gate * (1.0 - sigma)))

    def product(m, lth, ltl, rh, rl):
        @pl.loop(0, 4)
        def _(i):
            rows = pl.ds(pl.multiple_of(i * 128, 128), 128)
            gp[m, rows, :] = mm3(lth[rows, :], ltl[rows, :], rh[...], rl[...])

    live = {}

    def begin(m):
        live[m] = [whole(m, s) for s in range(2)]
        for g in live[m]:
            next(g)

    def advance(m):
        for g in live[m]:
            next(g)

    product(1, kth, ktl, p3h, p3l)
    begin(1)
    product(0, kth, ktl, p1h, p1l)
    begin(0)
    advance(1)
    product(2, yth, ytl, hh, hl)
    begin(2)
    drive(live, lambda m: update(m, gf))

    def apply(load, store):
        @pl.loop(0, 2)
        def _(i):
            rows = pl.ds(pl.multiple_of(i * 256, 256), 256)
            ah, al = split(normalize(load(rows)))
            gate = mm3(ah, al, wh[0], wl[0])
            upper = mm3(ah, al, wh[1], wl[1])
            bh, bl = split(gate * jax.nn.sigmoid(gate) * upper)
            store(rows, normalize(mm3_nt(bh, bl, wh[2], wl[2])).astype(bf16))

    def keep_theirs(rows, v):
        o_mine[rows, :] = v.astype(f32)

    def keep_mine(rows, v):
        o_ref[rows, mine] = v

    apply(lambda r: q_got[r, :], keep_theirs)
    out = rcopy(o_mine, o_got, ex_s.at[3], ex_r.at[3], partner)
    out.start()
    apply(lambda r: q_ref[r, mine], keep_mine)
    out.wait_recv()
    o_ref[:, theirs] = o_got[...].astype(bf16)

    for c in swaps + [out] + sent:
        c.wait_send()

    @pl.when(block == 0)
    def _():
        for m in range(3):
            for s in range(2):
                shard(m, s).wait_send()


def chain(k, y, q, fast_init):
    dma = pltpu.SemaphoreType.DMA
    square = lambda n, t: pltpu.VMEM((n, N, N), t)
    tall = pltpu.VMEM((2 * N, N), bf16)
    wide = pltpu.VMEM((N, 2 * N), bf16)
    part = pltpu.VMEM((N, N), f32)
    vmem = pl.BlockSpec(memory_space=pltpu.VMEM)
    return pl.pallas_call(
        chain_kernel,
        out_shape=jax.ShapeDtypeStruct((N, 2 * N), bf16),
        in_specs=[vmem] * 4,
        out_specs=vmem,
        scratch_shapes=[
            part, part, part, part, part,
            tall, tall, wide, wide, tall, tall, wide, wide,
            tall, tall, tall, tall, tall, tall,
            square(3, f32), square(3, bf16), square(3, bf16), pltpu.VMEM((3, 1, N), f32),
            square(3, f32), square(3, f32), square(3, f32),
            pltpu.VMEM((3, 2, 6, 32, N), f32), pltpu.VMEM((3, 2, 6, 8, N), f32),
            dma((3, 2, 2, 6)), dma((3, 2, 2, 6)),
            dma((3, 2, 2, 4)), dma((3, 2, 2, 4)),
            dma((3, 2, 2, 4)), dma((3, 2, 2, 4)),
            dma((3, 2)), dma((3, 2)),
            dma((4,)), dma((4,)),
        ],
        compiler_params=pltpu.CompilerParams(
            collective_id=0, has_side_effects=True, vmem_limit_bytes=60 * 1024 * 1024
        ),
    )(k, y, q, fast_init)


def body(tokens, input_weight, rate_weight, fast_init, output_weight):
    flat = tokens[0]
    parts = jnp.transpose(input_weight, (1, 0, 2))
    q = dot(flat, parts[0])
    k = dot(flat, parts[1])
    rates = jax.nn.softplus(dot(flat, rate_weight))
    y = dot(flat, parts[2]).reshape(N, 2, N) * rates[:, :, None]
    joined = chain(k, y.reshape(N, 2 * N), q, fast_init)
    partial_out = dot(joined, output_weight)[None]
    return lax.psum_scatter(partial_out, "head", scatter_dimension=2, tiled=True).astype(bf16)


def solution(mesh):
    placed = (
        P("block", "tok", None),
        P(None, None, "head"),
        P(None, "head"),
        P("head", None, None, None),
        P("head", None),
    )
    return jax.shard_map(
        body, mesh=mesh, in_specs=placed, out_specs=P("block", "tok", "head"), check_vma=False
    )
```

time: 833 us -> 242 us (0.29)
  waiting for transfers between devices: 508 us -> 56.2 us
  blocking collectives: 132 us -> 0 us
  Pallas kernels: 0 us -> 128 us
  matrix products: 91.1 us -> 25 us
  local copies, waits for them, and re-layouts: 51 us -> 14.2 us
  other arithmetic: 28.1 us -> 2.72 us
    unnamed x7 -> x1, waiting for transfers between devices: 224 us -> 0.02 us
    ppermute x1 -> x0, waiting for transfers between devices: 138 us -> none  [passed_along(): return lax.ppermute(block, axis, route)]
    psum x2 -> x0, blocking collectives: 132 us -> none  [body(): total_sq = lax.psum(squares, 'tok')]
    pallas_call x0 -> x1, Pallas kernels: none -> 128 us  [chain(): pl.pallas_call(chain_kernel, out_shape=jax.ShapeDtypeStruct((N, 2 * N), b...]
    all_gather x2 -> x0, waiting for transfers between devices: 90.5 us -> none  [body(): weights = lax.all_gather(fresh, 'tok', axis=3, tiled=True)]
    dot_general x18 -> x5, matrix products: 91.1 us -> 25 us  [dot(): return jnp.dot(a, b, preferred_element_type=f32)]
    unnamed x23 -> x4, local copies, waits for them, and re-layouts: 24.5 us -> 0.01 us
    transpose x2 -> x0, local copies, waits for them, and re-layouts: 20.6 us -> none  [body(): partial_value = head_grads(weights, keys[local], targets[local])]
  transfers between devices with their start and end apart: 6 -> 1, of which waited for: 6 -> 1; matrix products, arithmetic and copies ran while one was open for 1% -> 0% of each run, Pallas kernels for 0% -> 0%
where the time goes in v1:
time: 242 us; the launch traced here: 240 us
  Pallas kernels  128 us (53%)
  waiting for transfers between devices  56.2 us (23%)
  matrix products  25 us (10%)
  local copies, waits for them, and re-layouts  14.2 us (6%)
  between operations  13.4 us (6%)
  other arithmetic  2.72 us (1%)
    pallas_call x1, Pallas kernels, chain(): pl.pallas_call(chain_kernel, out_shape=jax.ShapeDtypeStruct((N, 2 * N), b...  128 us
    reduce_scatter x1, waiting for transfers between devices, body(): lax.psum_scatter(partial_out, 'head', scatter_dimension=2, tiled=True)  56.2 us
    dot_general x5, matrix products, dot(): return jnp.dot(a, b, preferred_element_type=f32)  25 us
    dot_general x2, local copies, waits for them, and re-layouts, dot(): return jnp.dot(a, b, preferred_element_type=f32)  11.2 us
  transfers between devices with their start and end apart: 1, of which 1 were waited for; matrix products, arithmetic and copies ran while one was open for 0% of the time, Pallas kernels for 0%

profile of v1, /device:TPU:8, one launch (start us, length us, event | category | flops | bytes accessed | tf_op | source)
XLA Modules:
  0.0 239.7 jit_solution(6189468910958184101)
XLA Ops:
  6.5 0.0 copy-start
  6.5 0.0 reduce-scatter.2.cloned.1.call-start
  6.5 4.7 %slice_bitcast_fusion.2 = bf16[1024,2048]{0,1:T(8,128)(2,1)} fusion(bf16[3,2048,1024]{2,1,0:T(8,128)(2,1)} %bitcast.35), kind=kLoop, calls=%fused_computation.2 | loop fusion | bytes 8388608 | tf_op jit(solution)/shard_map/dot_general | solution.py:23
  11.2 0.0 copy-done
  11.3 5.8 %fusion.q_ref = f32[512,1024]{1,0:T(8,128)} fusion(bf16[3,2048,1024]{2,1,0:T(8,128)(2,1)} %bitcast.36, bf16[1,512,2048]{2,1,0:T(8,128)(2,1)S(1)} %copy-done), kind=kOutput, calls=%fused_computation.1 | convolution fusion | flops 2147483648 | bytes 8388608 | tf_op jit(solution)/shard_map/dot_general | solution.py:23
  17.1 5.9 %fusion.1.k_ref = f32[512,1024]{1,0:T(8,128)} fusion(bf16[3,2048,1024]{2,1,0:T(8,128)(2,1)} %bitcast.37, bf16[1,512,2048]{2,1,0:T(8,128)(2,1)S(1)} %copy-done), kind=kOutput, calls=%fused_computation.4 | convolution fusion | flops 2147483648 | bytes 8388608 | tf_op jit(solution)/shard_map/dot_general | solution.py:23
  23.0 0.0 copy-start.1
  23.0 6.5 %copy.6 = bf16[1024,2048]{1,0:T(8,128)(2,1)} copy(bf16[1024,2048]{0,1:T(8,128)(2,1)} %slice_bitcast_fusion.2) | data formatting | bytes 8388608 | tf_op jit(solution)/shard_map/dot_general | solution.py:23
  29.5 0.0 copy-done.1
  29.5 0.7 compare_select_fusion
  30.2 5.9 %fusion.8 = f32[512,2,512]{0,2,1:T(8,128)} fusion(bf16[2,512,2048]{2,1,0:T(8,128)(2,1)} %bitcast.33, bf16[1,512,2048]{2,1,0:T(8,128)(2,1)S(1)} %copy-done, f32[512,2]{0,1:T(2,128)S(1)} %compare_select_fusion), kind=kOutput, calls=%fused_computation.12 | convolution fusion | flops 2148007936 | bytes 8392704 | tf_op jit(solution)/shard_map/dot_general | solution.py:23
  36.0 2.9 %copy.8.y_ref = f32[512,1024]{1,0:T(8,128)} copy(f32[512,1024]{0,1:T(8,128)} %bitcast.34) | data formatting | bytes 4194304 | tf_op jit(solution)/shard_map/reshape | solution.py:362
  39.0 128.2 %shard_map.55 = bf16[512,1024]{1,0:T(8,128)(2,1)} custom-call(f32[512,1024]{1,0:T(8,128)} %fusion.1.k_ref, f32[512,1024]{1,0:T(8,128)} %copy.8.y_ref, f32[512,1024]{1,0:T(8,128)} %fusion.q_ref, bf16[2,3,512,512]{3,2,1,0:T(8,128)(2,1)} %w0_ref.1), custom_call_target="tpu_custom_call" | custom-call | tf_op jit(solution)/shard_map/pallas_call | solution.py:331
  167.2 6.8 %convolution_bitcast_fusion = f32[1,512,2048]{2,1,0:T(8,128)} fusion(bf16[512,1024]{1,0:T(8,128)(2,1)} %shard_map.55, bf16[1024,2048]{1,0:T(8,128)(2,1)} %param.9), kind=kOutput, calls=%fused_computation.5 | convolution fusion | flops 2147483648 | bytes 9437184 | tf_op jit(solution)/shard_map/dot_general | solution.py:23
  173.9 0.0 reduce-scatter.2.cloned.1.call-update
  174.0 56.2 %reduce-scatter.2.cloned.1.call-done = f32[1,512,1024]{2,1,0:T(8,128)} async-done(((f32[1,512,2048]{2,1,0:T(8,128)}), f32[1,512,1024]{2,1,0:T(8,128)}) %reduce-scatter.2.cloned.1.call-update) | async-done | bytes 2097168 | tf_op jit(solution)/shard_map/reduce_scatter | solution.py:364
  230.1 2.7 %convert_element_type.3 = bf16[1,512,1024]{2,1,0:T(8,128)(2,1)} convert(f32[1,512,1024]{2,1,0:T(8,128)} %reduce-scatter.2.cloned.1.call-done) | non-fusion elementwise | flops 524288 | bytes 3145728 | tf_op jit(solution)/shard_map/convert_element_type | solution.py:364
Async XLA Ops:
  6.5 4.7 %copy-start = (bf16[1,512,2048]{2,1,0:T(8,128)(2,1)S(1)}, bf16[1,512,2048]{2,1,0:T(8,128)(2,1)}, u32[]{:S(2)}) copy-start(bf16[1,512,2048]{2,1,0:T(8,128)(2,1)} %param.5) | copy-start | bytes 6291460
  6.5 223.6 %reduce-scatter.2.cloned.1.call-start = ((), (), s32[]{:S(2)}) async-start(), calls=%async_computation.1 | async-start | bytes 6291456 | tf_op jit(solution)/shard_map/reduce_scatter | solution.py:364
  23.0 6.5 %copy-start.1 = (bf16[2048,2]{0,1:T(2,128)(2,1)S(1)}, bf16[2048,2]{0,1:T(2,128)(2,1)}, u32[]{:S(2)}) copy-start(bf16[2048,2]{0,1:T(2,128)(2,1)} %param.7) | copy-start | bytes 24580
Sparse Core Ops, SparseCore 0:
  174.1 55.9 reduce-scatter.1

commit v2 on v1

--- a/solution.py
+++ b/solution.py
@@ -40,15 +40,16 @@
 
 
 def chain_kernel(
-    k_ref, y_ref, q_ref, w0_ref, o_ref,
-    k_got, y_got, q_got, o_mine, o_got,
-    kh, kl, kth, ktl, yh, yl, yth, ytl,
-    hh, hl, p3h, p3l, p1h, p1l,
+    tok_hbm, wi_hbm, rate_ref, w0_hbm, wo_hbm, o_ref,
+    tok_v, wo, w0, ks, ys, qs, qm, k_got, y_got, q_got, o_mine, o_got, o_all, p_got,
+    kh, kl, kth, ktl, yh, yl, yth, ytl, big,
     w, wh, wl, r0, gp, gf, gf1, r1, r2,
     rs_s, rs_r, ag_s, ag_r, a1_s, a1_r, sh_s, sh_r, ex_s, ex_r,
+    pt_s, pt_r, rl_s, rl_r, in_s, wi_s,
 ):
     tok = lax.axis_index("tok")
     block = lax.axis_index("block")
+    head = lax.axis_index("head")
     core = lax.rem(tok, 2)
     chip = lax.div(tok, 2)
     x = lax.rem(chip, 4)
@@ -62,9 +63,32 @@
 
     partner = {"tok": chip * 2 + (1 - core)}
     other_block = {"block": 1 - block}
+    diagonal = {"block": 1 - block, "head": 1 - head}
+    other_head = {"head": 1 - head}
+
+    mine = pl.ds(pl.multiple_of(core * N, N), N)
+    theirs = pl.ds(pl.multiple_of((1 - core) * N, N), N)
+
+    SEQ = ((1, theirs), (2, theirs), (1, mine), (2, mine), (0, theirs), (0, mine))
+
+    def weights(n):
+        part, columns = SEQ[n]
+        return pltpu.make_async_copy(wi_hbm.at[part, :, columns], big.at[n % 3], wi_s.at[n % 3])
+
+    load_tok = pltpu.make_async_copy(tok_hbm, tok_v, in_s.at[0])
+    load_w0 = pltpu.make_async_copy(w0_hbm.at[core], w0, in_s.at[1])
+    load_wo = pltpu.make_async_copy(wo_hbm, wo, in_s.at[2])
+    load_tok.start()
+    weights(0).start()
+    weights(1).start()
+    weights(2).start()
+    load_w0.start()
+    load_wo.start()
 
     barrier = pltpu.get_barrier_semaphore()
-    everyone = (partner, at_x(1), at_x(-1), at_z(1), at_z(-1), other_block)
+    everyone = (
+        partner, at_x(1), at_x(-1), at_z(1), at_z(-1), other_block, diagonal, other_head
+    )
     for device in everyone:
         pl.semaphore_signal(barrier, inc=1, device_id=device, device_id_type=MESH)
     pl.semaphore_wait(barrier, len(everyone))
@@ -75,42 +99,70 @@
             device_id=device, device_id_type=MESH,
         )
 
-    mine = pl.ds(pl.multiple_of(core * N, N), N)
-    theirs = pl.ds(pl.multiple_of((1 - core) * N, N), N)
     swaps = [
-        rcopy(src.at[:, theirs], dst, ex_s.at[n], ex_r.at[n], partner)
-        for n, (src, dst) in enumerate(((k_ref, k_got), (y_ref, y_got), (q_ref, q_got)))
+        rcopy(src, dst, ex_s.at[n], ex_r.at[n], partner)
+        for n, (src, dst) in enumerate(((ks, k_got), (ys, y_got), (qs, q_got)))
     ]
-    for copy in swaps:
-        copy.start()
-
+
+    def project(n, finish):
+        weights(n).wait()
+
+        @pl.loop(0, 2)
+        def _(i):
+            rows = pl.ds(pl.multiple_of(i * 256, 256), 256)
+            finish(i * 256, rows, dot(tok_v[rows, :], big[n % 3]))
+
+    def rates(rows, which):
+        r = rate_ref[rows, :]
+        return jnp.where(which == 0, r[:, 0:1], r[:, 1:2])
+
+    def prepare(base, rows, v, h_ref, l_ref, th_ref, tl_ref):
+        hi, lo = split(v)
+        to = pl.ds(pl.multiple_of(base, 256), 256)
+        h_ref[to, :] = hi
+        l_ref[to, :] = lo
+        th_ref[:, to] = hi.T
+        tl_ref[:, to] = lo.T
+
+    def put(ref, f):
+        def finish(base, rows, v):
+            ref[rows, :] = f(rows, v)
+
+        return finish
+
+    load_tok.wait()
+    project(0, put(ks, lambda r, v: normalize(v)))
+    swaps[0].start()
+    weights(3).start()
+    project(1, put(ys, lambda r, v: v * rates(r, 1 - core)))
+    swaps[1].start()
+    project(2, lambda b, r, v: prepare(b, r, normalize(v), kh, kl, kth, ktl))
+    project(3, lambda b, r, v: prepare(b, r, v * rates(r, core), yh, yl, yth, ytl))
+
+    def project_q():
+        weights(4).start()
+        weights(5).start()
+        project(4, put(qs, lambda r, v: normalize(v)))
+        swaps[2].start()
+        project(5, put(qm, lambda r, v: normalize(v)))
+
+    load_w0.wait()
     for m in range(3):
-        start = w0_ref[core, m].astype(f32)
+        start = w0[m].astype(f32)
         w[m] = start
         wh[m], wl[m] = split(start)
         r0[m] = jnp.sqrt(jnp.mean(start * start, axis=0, keepdims=True))
 
-    def prepare(load, base, scale, h_ref, l_ref, th_ref, tl_ref):
+    def prepare_got(got, h_ref, l_ref, th_ref, tl_ref):
         @pl.loop(0, 2)
         def _(i):
             rows = pl.ds(pl.multiple_of(i * 256, 256), 256)
-            v = load(rows)
-            if scale:
-                v = normalize(v)
-            hi, lo = split(v)
-            to = pl.ds(pl.multiple_of(base + i * 256, 256), 256)
-            h_ref[to, :] = hi
-            l_ref[to, :] = lo
-            th_ref[:, to] = hi.T
-            tl_ref[:, to] = lo.T
-
-    prepare(lambda r: k_ref[r, mine], 0, True, kh, kl, kth, ktl)
-    prepare(lambda r: y_ref[r, mine], 0, False, yh, yl, yth, ytl)
+            prepare(N + i * 256, rows, got[rows, :], h_ref, l_ref, th_ref, tl_ref)
+
     swaps[0].wait_recv()
-    prepare(lambda r: k_got[r, :], N, True, kh, kl, kth, ktl)
+    prepare_got(k_got, kh, kl, kth, ktl)
     swaps[1].wait_recv()
-    prepare(lambda r: y_got[r, :], N, False, yh, yl, yth, ytl)
-    swaps[2].wait_recv()
+    prepare_got(y_got, yh, yl, yth, ytl)
 
     def rows_of(s, j1, j2=None, off=0, count=64):
         at = s * 256 + j1 * 64 + off
@@ -212,14 +264,31 @@
         yield from gather(gf, m, s, ag_s, ag_r, sent)
 
     def update(m, g_ref):
-        g = g_ref[m]
-        total = jnp.sum(jnp.sum(g * g, axis=0, keepdims=True), axis=1, keepdims=True)
+        def rows_at(i):
+            return pl.ds(pl.multiple_of(i * 64, 64), 64)
+
+        def squares(i, total):
+            g = g_ref[m, rows_at(i), :]
+            return total + jnp.sum(g * g, axis=0, keepdims=True)
+
+        total = jnp.sum(lax.fori_loop(0, 8, squares, jnp.zeros((1, N), f32)), axis=1, keepdims=True)
         scale = step_size / jnp.sqrt(total / (N * N) + epsilon)
-        moved = w[m] + g * scale
-        column = jnp.mean(moved * moved, axis=0, keepdims=True)
-        fresh = moved * (r0[m] / jnp.sqrt(column + epsilon))
-        w[m] = fresh
-        wh[m], wl[m] = split(fresh)
+
+        def move(i, column):
+            rows = rows_at(i)
+            moved = w[m, rows, :] + g_ref[m, rows, :] * scale
+            w[m, rows, :] = moved
+            return column + jnp.sum(moved * moved, axis=0, keepdims=True)
+
+        column = lax.fori_loop(0, 8, move, jnp.zeros((1, N), f32)) / N
+        factor = r0[m] / jnp.sqrt(column + epsilon)
+
+        @pl.loop(0, 8)
+        def _(i):
+            rows = rows_at(i)
+            fresh = w[m, rows, :] * factor
+            w[m, rows, :] = fresh
+            wh[m, rows, :], wl[m, rows, :] = split(fresh)
 
     def drive(streams, finish):
         left = {m: list(streams[m]) for m in streams}
@@ -239,6 +308,7 @@
 
     @pl.when(block == 1)
     def _():
+        project_q()
         done = []
 
         def first(m, s):
@@ -248,6 +318,10 @@
         drive({m: [first(m, s) for s in range(2)] for m in range(3)}, lambda m: update(m, gf1))
         for c in done:
             c.wait_send()
+
+    hh, hl = big.at[0, pl.ds(0, 2 * N)], big.at[0, pl.ds(2 * N, 2 * N)]
+    p3h, p3l = big.at[1, pl.ds(0, 2 * N)], big.at[1, pl.ds(2 * N, 2 * N)]
+    p1h, p1l = big.at[2, pl.ds(0, 2 * N)], big.at[2, pl.ds(2 * N, 2 * N)]
 
     @pl.loop(0, 4)
     def _(i):
@@ -288,11 +362,15 @@
     begin(2)
     drive(live, lambda m: update(m, gf))
 
+    @pl.when(block == 0)
+    def _():
+        project_q()
+
     def apply(load, store):
         @pl.loop(0, 2)
         def _(i):
             rows = pl.ds(pl.multiple_of(i * 256, 256), 256)
-            ah, al = split(normalize(load(rows)))
+            ah, al = split(load(rows))
             gate = mm3(ah, al, wh[0], wl[0])
             upper = mm3(ah, al, wh[1], wl[1])
             bh, bl = split(gate * jax.nn.sigmoid(gate) * upper)
@@ -302,16 +380,94 @@
         o_mine[rows, :] = v.astype(f32)
 
     def keep_mine(rows, v):
-        o_ref[rows, mine] = v
-
+        o_all[rows, mine] = v
+
+    swaps[2].wait_recv()
     apply(lambda r: q_got[r, :], keep_theirs)
     out = rcopy(o_mine, o_got, ex_s.at[3], ex_r.at[3], partner)
     out.start()
-    apply(lambda r: q_ref[r, mine], keep_mine)
+    apply(lambda r: qm[r, :], keep_mine)
+    for c in sent:
+        c.wait_send()
+    load_wo.wait()
     out.wait_recv()
-    o_ref[:, theirs] = o_got[...].astype(bf16)
-
-    for c in swaps + [out] + sent:
+    o_all[:, theirs] = o_got[...].astype(bf16)
+
+    own_half = pl.ds(pl.multiple_of(head * 2 * N, 2 * N), 2 * N)
+    far_half = pl.ds(pl.multiple_of((1 - head) * 2 * N, 2 * N), 2 * N)
+
+    def piece(j):
+        return pl.ds(0, 2), pl.ds(pl.multiple_of(j * 32, 32), 32)
+
+    def direct(j):
+        c, r = piece(j)
+        return rcopy(gp.at[c, r], p_got.at[c, r], pt_s.at[j], pt_r.at[j], other_head)
+
+    def first_leg(j, device):
+        c, r = piece(j)
+        return rcopy(gp.at[c, r], gf1.at[c, r], rl_s.at[j], rl_r.at[j], device)
+
+    def second_leg(j, device):
+        c, r = piece(j)
+        return rcopy(gf1.at[c, r], p_got.at[c, r], pt_s.at[j], pt_r.at[j], device)
+
+    @pl.loop(0, 4)
+    def _(i):
+        rows = pl.ds(pl.multiple_of(i * 128, 128), 128)
+        v = dot(o_all[rows, :], wo[:, far_half])
+        gp[0, rows, :] = v[:, :N]
+        gp[1, rows, :] = v[:, N:]
+
+        @pl.when(block == 0)
+        def _():
+            for j in range(4):
+                direct(i * 4 + j).start()
+
+        @pl.when(block == 1)
+        def _():
+            for j in range(2):
+                first_leg(i * 4 + 2 * j, other_block).start()
+                first_leg(i * 4 + 2 * j + 1, diagonal).start()
+
+    @pl.loop(0, 4)
+    def _(i):
+        rows = pl.ds(pl.multiple_of(i * 128, 128), 128)
+        v = dot(o_all[rows, :], wo[:, own_half])
+        w[0, rows, :] = v[:, :N]
+        w[1, rows, :] = v[:, N:]
+
+    @pl.loop(0, 16)
+    def _(j):
+        direct(j).wait_recv()
+        _, rows = piece(j)
+        for half in range(2):
+            v = w[half, rows, :] + p_got[half, rows, :]
+            o_ref[rows, pl.ds(half * N, N)] = v.astype(bf16)
+
+    @pl.when(block == 0)
+    def _():
+        @pl.loop(0, 16)
+        def _(j):
+            direct(j).wait_send()
+
+        @pl.loop(0, 8)
+        def _(j):
+            first_leg(2 * j, other_block).wait_recv()
+            second_leg(2 * j, diagonal).start()
+            first_leg(2 * j + 1, diagonal).wait_recv()
+            second_leg(2 * j + 1, other_block).start()
+
+        @pl.loop(0, 16)
+        def _(j):
+            second_leg(j, diagonal).wait_send()
+
+    @pl.when(block == 1)
+    def _():
+        @pl.loop(0, 16)
+        def _(j):
+            first_leg(j, diagonal).wait_send()
+
+    for c in swaps + [out]:
         c.wait_send()
 
     @pl.when(block == 0)
@@ -321,22 +477,24 @@
                 shard(m, s).wait_send()
 
 
-def chain(k, y, q, fast_init):
+def chain(tokens, weight, rates, fast_init, output_weight):
     dma = pltpu.SemaphoreType.DMA
     square = lambda n, t: pltpu.VMEM((n, N, N), t)
     tall = pltpu.VMEM((2 * N, N), bf16)
     wide = pltpu.VMEM((N, 2 * N), bf16)
     part = pltpu.VMEM((N, N), f32)
     vmem = pl.BlockSpec(memory_space=pltpu.VMEM)
+    hbm = pl.BlockSpec(memory_space=pl.ANY)
     return pl.pallas_call(
         chain_kernel,
         out_shape=jax.ShapeDtypeStruct((N, 2 * N), bf16),
-        in_specs=[vmem] * 4,
+        in_specs=[hbm, hbm, vmem, hbm, hbm],
         out_specs=vmem,
         scratch_shapes=[
-            part, part, part, part, part,
-            tall, tall, wide, wide, tall, tall, wide, wide,
-            tall, tall, tall, tall, tall, tall,
+            pltpu.VMEM((N, 4 * N), bf16), pltpu.VMEM((2 * N, 4 * N), bf16), square(3, bf16),
+            part, part, part, part, part, part, part, part, part,
+            pltpu.VMEM((N, 2 * N), bf16), square(2, f32),
+            tall, tall, wide, wide, tall, tall, wide, wide, pltpu.VMEM((3, 4 * N, N), bf16),
             square(3, f32), square(3, bf16), square(3, bf16), pltpu.VMEM((3, 1, N), f32),
             square(3, f32), square(3, f32), square(3, f32),
             pltpu.VMEM((3, 2, 6, 32, N), f32), pltpu.VMEM((3, 2, 6, 8, N), f32),
@@ -345,23 +503,19 @@
             dma((3, 2, 2, 4)), dma((3, 2, 2, 4)),
             dma((3, 2)), dma((3, 2)),
             dma((4,)), dma((4,)),
+            dma((16,)), dma((16,)), dma((16,)), dma((16,)), dma((3,)), dma((3,)),
         ],
         compiler_params=pltpu.CompilerParams(
-            collective_id=0, has_side_effects=True, vmem_limit_bytes=60 * 1024 * 1024
+            collective_id=0, has_side_effects=True, vmem_limit_bytes=62 * 1024 * 1024
         ),
-    )(k, y, q, fast_init)
+    )(tokens, weight, rates, fast_init, output_weight)
 
 
 def body(tokens, input_weight, rate_weight, fast_init, output_weight):
     flat = tokens[0]
-    parts = jnp.transpose(input_weight, (1, 0, 2))
-    q = dot(flat, parts[0])
-    k = dot(flat, parts[1])
     rates = jax.nn.softplus(dot(flat, rate_weight))
-    y = dot(flat, parts[2]).reshape(N, 2, N) * rates[:, :, None]
-    joined = chain(k, y.reshape(N, 2 * N), q, fast_init)
-    partial_out = dot(joined, output_weight)[None]
-    return lax.psum_scatter(partial_out, "head", scatter_dimension=2, tiled=True).astype(bf16)
+    mixed = chain(flat, jnp.transpose(input_weight, (1, 0, 2)), rates, fast_init, output_weight)
+    return mixed[None]
 
 
 def solution(mesh):

time: 242 us -> 164 us (0.68)
  waiting for transfers between devices: 56.2 us -> 0 us
  Pallas kernels: 128 us -> 158 us
  matrix products: 25 us -> 3 us
  between operations: 13.4 us -> 0.01 us
  local copies, waits for them, and re-layouts: 14.2 us -> 2.96 us
  other arithmetic: 2.72 us -> 0 us
    reduce_scatter x1 -> x0, waiting for transfers between devices: 56.2 us -> none  [body(): lax.psum_scatter(partial_out, 'head', scatter_dimension=2, tiled=True)]
    pallas_call x1, Pallas kernels: 128 us -> 158 us  [chain(): pl.pallas_call(chain_kernel, out_shape=jax.ShapeDtypeStruct((N, 2 * N), b...]
    dot_general x5 -> x1, matrix products: 25 us -> 3 us  [dot(): return jnp.dot(a, b, preferred_element_type=f32)]
    dot_general x2 -> x0, local copies, waits for them, and re-layouts: 11.2 us -> none  [dot(): return jnp.dot(a, b, preferred_element_type=f32)]
    unnamed x4 -> x3, local copies, waits for them, and re-layouts: 0.01 us -> 2.96 us
    reshape x1 -> x0, local copies, waits for them, and re-layouts: 2.93 us -> none  [body(): joined = chain(k, y.reshape(N, 2 * N), q, fast_init)]
    convert_element_type x1 -> x0, other arithmetic: 2.72 us -> none  [body(): lax.psum_scatter(partial_out, 'head', scatter_dimension=2, tiled=True)]
  transfers between devices with their start and end apart: 1 -> 0, of which waited for: 1 -> 0; matrix products, arithmetic and copies ran while one was open for 0% -> 0% of each run, Pallas kernels for 0% -> 0%
where the time goes in v2:
time: 164 us
  Pallas kernels  158 us (96%)
  matrix products  3 us (2%)
  local copies, waits for them, and re-layouts  2.96 us (2%)
    pallas_call x1, Pallas kernels, chain(): pl.pallas_call(chain_kernel, out_shape=jax.ShapeDtypeStruct((N, 2 * N), b...  158 us

profile of v2, /device:TPU:8, one launch (start us, length us, event | category | flops | bytes accessed | tf_op | source)
XLA Modules:
  0.0 164.0 jit_solution(1856397994234291926)
XLA Ops:
  0.0 0.0 copy-start
  0.0 0.7 copy-done
  0.7 3.0 %compare_select_fusion.rate_ref = f32[512,2]{1,0:T(8,128)} fusion(bf16[2048,2]{0,1:T(2,128)(2,1)S(1)} %copy-done, bf16[1,512,2048]{2,1,0:T(8,128)(2,1)} %param.5), kind=kOutput, calls=%fused_computation | convolution fusion | flops 4200448 | bytes 2109440 | tf_op jit(solution)/shard_map/dot_general | solution.py:23
  3.7 158.0 %shard_map.55 = bf16[512,1024]{1,0:T(8,128)(2,1)} custom-call(bf16[512,2048]{1,0:T(8,128)(2,1)} %bitcast.10, bf16[3,2048,1024]{2,1,0:T(8,128)(2,1)} %bitcast.8, f32[512,2]{1,0:T(8,128)} %compare_select_fusion.rate_ref, bf16[2,3,512,512]{3,2,1,0:T(8,128)(2,1)} %w0_hbm.1, bf16[1024,2048]{1,0:T(8,128)(2,1)} %wo_hbm.1), custom_call_target="tpu_custom_call" | custom-call | tf_op jit(solution)/shard_map/pallas_call | solution.py:488
  161.8 2.3 %copy.19 = bf16[1,512,1024]{2,1,0:T(8,128)(2,1)} copy(bf16[1,512,1024]{2,1,0:T(8,128)(2,1)} %bitcast.9) | data formatting | bytes 2097152
Async XLA Ops:
  0.0 0.7 copy-start

commit v3 on v2

--- a/solution.py
+++ b/solution.py
@@ -113,7 +113,7 @@
             finish(i * 256, rows, dot(tok_v[rows, :], big[n % 3]))
 
     def rates(rows, which):
-        r = rate_ref[rows, :]
+        r = jax.nn.softplus(dot_nt(tok_v[rows, :], rate_ref[...]))
         return jnp.where(which == 0, r[:, 0:1], r[:, 1:2])
 
     def prepare(base, rows, v, h_ref, l_ref, th_ref, tl_ref):
@@ -170,7 +170,7 @@
             at = at + j2 * 16
         return pl.ds(pl.multiple_of(at, 8), count)
 
-    def reduce_stage(m, piece, n, got, store, i, go, ss, rs):
+    def reduce_stage(m, piece, n, got, store, i, go, ss, rs, sent):
         src = gp.at[m]
         nxt, prv, far = lax.rem(i + 1, 4), lax.rem(i + 3, 4), lax.rem(i + 2, 4)
         right, left = go(1), go(-1)
@@ -237,9 +237,7 @@
         rows = rows_of(s, i1, i2, 0, 16)
         return rcopy(gf.at[m, rows], gf1.at[m, rows], sh_s.at[m, s], sh_r.at[m, s], other_block)
 
-    sent = []
-
-    def whole(m, s):
+    def reduce(m, s, sent):
         i1, go1, i2, go2 = axes[s]
 
         def store1(o, v):
@@ -250,17 +248,20 @@
 
         yield from reduce_stage(
             m, lambda j, o, c: rows_of(s, j, None, o, c), 32, r1.at[m, s], store1, i1, go1,
-            rs_s.at[m, s, 0], rs_r.at[m, s, 0],
+            rs_s.at[m, s, 0], rs_r.at[m, s, 0], sent,
         )
         yield from reduce_stage(
             m, lambda j, o, c: rows_of(s, i1, j, o, c), 8, r2.at[m, s], store2, i2, go2,
-            rs_s.at[m, s, 1], rs_r.at[m, s, 1],
+            rs_s.at[m, s, 1], rs_r.at[m, s, 1], sent,
         )
 
-        @pl.when(block == 0)
-        def _():
-            shard(m, s).start()
-
+    def first_block(m, s, sent):
+        yield from reduce(m, s, sent)
+        shard(m, s).start()
+        sent.append(shard(m, s))
+
+    def last_block(m, s, sent):
+        yield from reduce(m, s, sent)
         yield from gather(gf, m, s, ag_s, ag_r, sent)
 
     def update(m, g_ref):
@@ -342,25 +343,44 @@
             rows = pl.ds(pl.multiple_of(i * 128, 128), 128)
             gp[m, rows, :] = mm3(lth[rows, :], ltl[rows, :], rh[...], rl[...])
 
-    live = {}
-
-    def begin(m):
-        live[m] = [whole(m, s) for s in range(2)]
-        for g in live[m]:
-            next(g)
-
-    def advance(m):
-        for g in live[m]:
-            next(g)
-
-    product(1, kth, ktl, p3h, p3l)
-    begin(1)
-    product(0, kth, ktl, p1h, p1l)
-    begin(0)
-    advance(1)
-    product(2, yth, ytl, hh, hl)
-    begin(2)
-    drive(live, lambda m: update(m, gf))
+    def exchange(stream, finish, sent):
+        live = {}
+
+        def begin(m):
+            live[m] = [stream(m, s, sent) for s in range(2)]
+            for g in live[m]:
+                next(g)
+
+        def advance(m):
+            for g in live[m]:
+                next(g)
+
+        product(1, kth, ktl, p3h, p3l)
+        begin(1)
+        product(0, kth, ktl, p1h, p1l)
+        begin(0)
+        advance(1)
+        product(2, yth, ytl, hh, hl)
+        begin(2)
+        drive(live, finish)
+
+    @pl.when(block == 0)
+    def _():
+        sent = []
+        exchange(first_block, lambda m: None, sent)
+        drive(
+            {m: [gather(gf, m, s, ag_s, ag_r, sent) for s in range(2)] for m in range(3)},
+            lambda m: update(m, gf),
+        )
+        for c in sent:
+            c.wait_send()
+
+    @pl.when(block == 1)
+    def _():
+        sent = []
+        exchange(last_block, lambda m: update(m, gf), sent)
+        for c in sent:
+            c.wait_send()
 
     @pl.when(block == 0)
     def _():
@@ -387,8 +407,6 @@
     out = rcopy(o_mine, o_got, ex_s.at[3], ex_r.at[3], partner)
     out.start()
     apply(lambda r: qm[r, :], keep_mine)
-    for c in sent:
-        c.wait_send()
     load_wo.wait()
     out.wait_recv()
     o_all[:, theirs] = o_got[...].astype(bf16)
@@ -470,14 +488,8 @@
     for c in swaps + [out]:
         c.wait_send()
 
-    @pl.when(block == 0)
-    def _():
-        for m in range(3):
-            for s in range(2):
-                shard(m, s).wait_send()
-
-
-def chain(tokens, weight, rates, fast_init, output_weight):
+
+def chain(tokens, weight, rate_weight, fast_init, output_weight):
     dma = pltpu.SemaphoreType.DMA
     square = lambda n, t: pltpu.VMEM((n, N, N), t)
     tall = pltpu.VMEM((2 * N, N), bf16)
@@ -508,13 +520,14 @@
         compiler_params=pltpu.CompilerParams(
             collective_id=0, has_side_effects=True, vmem_limit_bytes=62 * 1024 * 1024
         ),
-    )(tokens, weight, rates, fast_init, output_weight)
+    )(tokens, weight, rate_weight, fast_init, output_weight)
 
 
 def body(tokens, input_weight, rate_weight, fast_init, output_weight):
     flat = tokens[0]
-    rates = jax.nn.softplus(dot(flat, rate_weight))
-    mixed = chain(flat, jnp.transpose(input_weight, (1, 0, 2)), rates, fast_init, output_weight)
+    mixed = chain(
+        flat, jnp.transpose(input_weight, (1, 0, 2)), rate_weight.T, fast_init, output_weight
+    )
     return mixed[None]
 
 

time: 164 us -> 164 us (level)
  matrix products: 3 us -> 0 us
  Pallas kernels: 158 us -> 161 us
    pallas_call x1, Pallas kernels: 158 us -> 161 us  [chain(): pl.pallas_call(chain_kernel, out_shape=jax.ShapeDtypeStruct((N, 2 * N), b...]
    dot_general x1 -> x0, matrix products: 3 us -> none  [dot(): return jnp.dot(a, b, preferred_element_type=f32)]
where the time goes in v3:
time: 164 us
  Pallas kernels  161 us (98%)
  local copies, waits for them, and re-layouts  2.26 us (1%)
    pallas_call x1, Pallas kernels, chain(): pl.pallas_call(chain_kernel, out_shape=jax.ShapeDtypeStruct((N, 2 * N), b...  161 us

profile of v3, /device:TPU:8, one launch (start us, length us, event | category | flops | bytes accessed | tf_op | source)
XLA Modules:
  0.0 163.7 jit_solution(9907814550853501008)
XLA Ops:
  0.0 161.5 %shard_map.55 = bf16[512,1024]{1,0:T(8,128)(2,1)} custom-call(bf16[512,2048]{1,0:T(8,128)(2,1)} %bitcast.6, bf16[3,2048,1024]{2,1,0:T(8,128)(2,1)} %bitcast.4, bf16[2,2048]{1,0:T(2,128)(2,1)} %bitcast.7, bf16[2,3,512,512]{3,2,1,0:T(8,128)(2,1)} %w0_hbm.1, bf16[1024,2048]{1,0:T(8,128)(2,1)} %wo_hbm.1), custom_call_target="tpu_custom_call" | custom-call | tf_op jit(solution)/shard_map/pallas_call | solution.py:500
  161.5 2.3 %copy.7 = bf16[1,512,1024]{2,1,0:T(8,128)(2,1)} copy(bf16[1,512,1024]{2,1,0:T(8,128)(2,1)} %bitcast.5) | data formatting | bytes 2097152

commit v4 on v3

--- a/solution.py
+++ b/solution.py
@@ -41,11 +41,11 @@
 
 def chain_kernel(
     tok_hbm, wi_hbm, rate_ref, w0_hbm, wo_hbm, o_ref,
-    tok_v, wo, w0, ks, ys, qs, qm, k_got, y_got, q_got, o_mine, o_got, o_all, p_got,
+    tok_v, wo, w0, ks, ys, qs, qm, k_got, y_got, q_got, o_got, o_all, o_far, seed, seed32, wog, wos,
     kh, kl, kth, ktl, yh, yl, yth, ytl, big,
     w, wh, wl, r0, gp, gf, gf1, r1, r2,
     rs_s, rs_r, ag_s, ag_r, a1_s, a1_r, sh_s, sh_r, ex_s, ex_r,
-    pt_s, pt_r, rl_s, rl_r, in_s, wi_s,
+    pt_s, pt_r, rl_s, rl_r, sd_s, sd_r, wg_s, wg_r, in_s, wi_s,
 ):
     tok = lax.axis_index("tok")
     block = lax.axis_index("block")
@@ -77,17 +77,34 @@
 
     load_tok = pltpu.make_async_copy(tok_hbm, tok_v, in_s.at[0])
     load_w0 = pltpu.make_async_copy(w0_hbm.at[core], w0, in_s.at[1])
-    load_wo = pltpu.make_async_copy(wo_hbm, wo, in_s.at[2])
+    own_half = pl.ds(pl.multiple_of(head * 2 * N, 2 * N), 2 * N)
+    far_half = pl.ds(pl.multiple_of((1 - head) * 2 * N, 2 * N), 2 * N)
+    load_wo = [
+        pltpu.make_async_copy(wo_hbm.at[pl.ds(n * N, N), own_half], wo.at[n], in_s.at[2 + n])
+        for n in range(2)
+    ]
+    seed_at = ((x * 64 + z * 16), (256 + z * 64 + x * 16))
+    load_seed = [
+        pltpu.make_async_copy(
+            wo_hbm.at[pl.ds(pl.multiple_of(core * N + seed_at[n], 16), 16), far_half],
+            seed.at[n], in_s.at[4 + n],
+        )
+        for n in range(2)
+    ]
+    for copy in load_seed:
+        copy.start()
     load_tok.start()
     weights(0).start()
     weights(1).start()
     weights(2).start()
     load_w0.start()
-    load_wo.start()
+    for copy in load_wo:
+        copy.start()
 
     barrier = pltpu.get_barrier_semaphore()
     everyone = (
-        partner, at_x(1), at_x(-1), at_z(1), at_z(-1), other_block, diagonal, other_head
+        partner, at_x(1), at_x(-1), at_z(1), at_z(-1), other_block, diagonal, other_head,
+        {**other_block, **partner}, {**diagonal, **partner}, {**other_head, **partner},
     )
     for device in everyone:
         pl.semaphore_signal(barrier, inc=1, device_id=device, device_id_type=MESH)
@@ -130,14 +147,88 @@
 
         return finish
 
+    def rows_of(s, j1, j2=None, off=0, count=64):
+        at = s * 256 + j1 * 64 + off
+        if j2 is not None:
+            at = at + j2 * 16
+        return pl.ds(pl.multiple_of(at, 8), count)
+
+    def gather_stage(buf, piece, n, i, go, ss, rs, done):
+        nxt, prv, far = lax.rem(i + 1, 4), lax.rem(i + 3, 4), lax.rem(i + 2, 4)
+        right, left = go(1), go(-1)
+
+        def send(k, rows, device):
+            return rcopy(buf.at[rows], buf.at[rows], ss.at[k], rs.at[k], device)
+
+        c0 = send(0, piece(i, 0, 2 * n), right)
+        c1 = send(1, piece(i, 0, 2 * n), left)
+        c0.start()
+        c1.start()
+        yield
+        send(0, piece(prv, 0, 2 * n), right).wait_recv()
+        c2 = send(2, piece(prv, 0, n), right)
+        c2.start()
+        send(1, piece(nxt, 0, 2 * n), left).wait_recv()
+        c3 = send(3, piece(nxt, n, n), left)
+        c3.start()
+        yield
+        send(2, piece(far, 0, n), right).wait_recv()
+        send(3, piece(far, n, n), left).wait_recv()
+        done.extend((c0, c1, c2, c3))
+
+    axes = ((x, at_x, z, at_z), (z, at_z, x, at_x))
+
+    def gather(buf, m, s, ss, rs, done):
+        i1, go1, i2, go2 = axes[s]
+        yield from gather_stage(
+            buf.at[m], lambda j, o, c: rows_of(s, i1, j, o, c), 8, i2, go2,
+            ss.at[m, s, 0], rs.at[m, s, 0], done,
+        )
+        yield from gather_stage(
+            buf.at[m], lambda j, o, c: rows_of(s, j, None, o, c), 32, i1, go1,
+            ss.at[m, s, 1], rs.at[m, s, 1], done,
+        )
+
+    SHARDS = tuple((m, n) for m in range(2) for n in range(2))
+    seeds = [
+        rcopy(
+            seed32.at[m, n], wog.at[m, pl.ds(pl.multiple_of(seed_at[n], 16), 16)],
+            sd_s.at[m, n], sd_r.at[m, n], diagonal,
+        )
+        for m, n in SHARDS
+    ]
+    for copy in load_seed:
+        copy.wait()
+    for m, n in SHARDS:
+        seed32[m, n] = seed[n, :, m * N:(m + 1) * N].astype(f32)
+    for copy in seeds:
+        copy.start()
+    wo_sent = []
+
+    def bring_weights(m, n):
+        seeds[m * 2 + n].wait_recv()
+        yield from gather(wog, m, n, wg_s, wg_r, wo_sent)
+
+    bringing = [bring_weights(m, n) for m, n in SHARDS]
+
+    def bring():
+        for g in bringing:
+            next(g, None)
+
+    wo_swap = rcopy(wog, wos, ex_s.at[5], ex_r.at[5], partner)
+
     load_tok.wait()
     project(0, put(ks, lambda r, v: normalize(v)))
     swaps[0].start()
     weights(3).start()
+    bring()
     project(1, put(ys, lambda r, v: v * rates(r, 1 - core)))
     swaps[1].start()
+    bring()
     project(2, lambda b, r, v: prepare(b, r, normalize(v), kh, kl, kth, ktl))
+    bring()
     project(3, lambda b, r, v: prepare(b, r, v * rates(r, core), yh, yl, yth, ytl))
+    bring()
 
     def project_q():
         weights(4).start()
@@ -161,14 +252,22 @@
 
     swaps[0].wait_recv()
     prepare_got(k_got, kh, kl, kth, ktl)
+    bring()
     swaps[1].wait_recv()
     prepare_got(y_got, yh, yl, yth, ytl)
-
-    def rows_of(s, j1, j2=None, off=0, count=64):
-        at = s * 256 + j1 * 64 + off
-        if j2 is not None:
-            at = at + j2 * 16
-        return pl.ds(pl.multiple_of(at, 8), count)
+    bring()
+    wo_swap.start()
+
+    def keep_weights():
+        wo_swap.wait_recv()
+
+        @pl.loop(0, 4)
+        def _(i):
+            rows = pl.ds(pl.multiple_of(i * 128, 128), 128)
+            for m in range(2):
+                columns = pl.ds(m * N, N)
+                wo[2 + core, rows, columns] = wog[m, rows, :].astype(bf16)
+                wo[3 - core, rows, columns] = wos[m, rows, :].astype(bf16)
 
     def reduce_stage(m, piece, n, got, store, i, go, ss, rs, sent):
         src = gp.at[m]
@@ -196,42 +295,6 @@
         store(n, gp[m, piece(i, n, n), :] + got[2] + got[5])
         sent.extend((c0, c1, c2, c3, c4, c5))
 
-    def gather_stage(buf, piece, n, i, go, ss, rs, done):
-        nxt, prv, far = lax.rem(i + 1, 4), lax.rem(i + 3, 4), lax.rem(i + 2, 4)
-        right, left = go(1), go(-1)
-
-        def send(k, rows, device):
-            return rcopy(buf.at[rows], buf.at[rows], ss.at[k], rs.at[k], device)
-
-        c0 = send(0, piece(i, 0, 2 * n), right)
-        c1 = send(1, piece(i, 0, 2 * n), left)
-        c0.start()
-        c1.start()
-        yield
-        send(0, piece(prv, 0, 2 * n), right).wait_recv()
-        c2 = send(2, piece(prv, 0, n), right)
-        c2.start()
-        send(1, piece(nxt, 0, 2 * n), left).wait_recv()
-        c3 = send(3, piece(nxt, n, n), left)
-        c3.start()
-        yield
-        send(2, piece(far, 0, n), right).wait_recv()
-        send(3, piece(far, n, n), left).wait_recv()
-        done.extend((c0, c1, c2, c3))
-
-    axes = ((x, at_x, z, at_z), (z, at_z, x, at_x))
-
-    def gather(buf, m, s, ss, rs, done):
-        i1, go1, i2, go2 = axes[s]
-        yield from gather_stage(
-            buf.at[m], lambda j, o, c: rows_of(s, i1, j, o, c), 8, i2, go2,
-            ss.at[m, s, 0], rs.at[m, s, 0], done,
-        )
-        yield from gather_stage(
-            buf.at[m], lambda j, o, c: rows_of(s, j, None, o, c), 32, i1, go1,
-            ss.at[m, s, 1], rs.at[m, s, 1], done,
-        )
-
     def shard(m, s):
         i1, _, i2, _ = axes[s]
         rows = rows_of(s, i1, i2, 0, 16)
@@ -310,6 +373,7 @@
     @pl.when(block == 1)
     def _():
         project_q()
+        keep_weights()
         done = []
 
         def first(m, s):
@@ -368,10 +432,13 @@
     def _():
         sent = []
         exchange(first_block, lambda m: None, sent)
-        drive(
-            {m: [gather(gf, m, s, ag_s, ag_r, sent) for s in range(2)] for m in range(3)},
-            lambda m: update(m, gf),
-        )
+        live = {m: [gather(gf, m, s, ag_s, ag_r, sent) for s in range(2)] for m in range(3)}
+        for m in ORDER:
+            for g in live[m]:
+                next(g)
+        project_q()
+        keep_weights()
+        drive(live, lambda m: update(m, gf))
         for c in sent:
             c.wait_send()
 
@@ -382,110 +449,138 @@
         for c in sent:
             c.wait_send()
 
-    @pl.when(block == 0)
-    def _():
-        project_q()
-
-    def apply(load, store):
+    def rows_at(j):
+        return pl.ds(pl.multiple_of(j * 64, 64), 64)
+
+    receivers = ({"tok": partner["tok"]}, {})
+
+    def direct(t, j):
+        r = rows_at(j)
+        device = {"head": 1 - head, **receivers[t]}
+        return rcopy(gp.at[t, r], o_far.at[core, r], pt_s.at[t, j], pt_r.at[t, j], device)
+
+    def arrival(t, j):
+        r = rows_at(j)
+        at = o_far.at[1 - core if t == 0 else core, r]
+        return rcopy(at, at, pt_s.at[t, j], pt_r.at[t, j], other_head)
+
+    def first_leg(t, j, device):
+        r = rows_at(j)
+        return rcopy(gp.at[t, r], gf1.at[t, r], rl_s.at[t, j], rl_r.at[t, j], device)
+
+    def second_leg(t, j, device):
+        r = rows_at(j)
+        return rcopy(
+            gf1.at[t, r], o_far.at[core, r], pt_s.at[t, 8 + j], pt_r.at[t, j],
+            {**device, **receivers[t]},
+        )
+
+    def send_far(t, i):
+        @pl.when(block == 0)
+        def _():
+            for j in range(4):
+                direct(t, i * 4 + j).start()
+
+        @pl.when(block == 1)
+        def _():
+            for j in range(0, 4, 2):
+                first_leg(t, i * 4 + j, other_block).start()
+                first_leg(t, i * 4 + j + 1, diagonal).start()
+
+    def give(i):
+        rows = pl.ds(pl.multiple_of(i * 256, 256), 256)
+        return rcopy(gp.at[0, rows], o_got.at[rows], ex_s.at[3 + i], ex_r.at[3 + i], partner)
+
+    def apply(t, q):
         @pl.loop(0, 2)
         def _(i):
             rows = pl.ds(pl.multiple_of(i * 256, 256), 256)
-            ah, al = split(load(rows))
+            ah, al = split(q[rows, :])
             gate = mm3(ah, al, wh[0], wl[0])
             upper = mm3(ah, al, wh[1], wl[1])
             bh, bl = split(gate * jax.nn.sigmoid(gate) * upper)
-            store(rows, normalize(mm3_nt(bh, bl, wh[2], wl[2])).astype(bf16))
-
-    def keep_theirs(rows, v):
-        o_mine[rows, :] = v.astype(f32)
-
-    def keep_mine(rows, v):
-        o_all[rows, mine] = v
+            o = normalize(mm3_nt(bh, bl, wh[2], wl[2])).astype(bf16)
+            gp[t, rows, :] = o.astype(f32)
+            if t == 1:
+                o_all[rows, mine] = o
+            send_far(t, i)
+            if t == 0:
+                give(i).start()
 
     swaps[2].wait_recv()
-    apply(lambda r: q_got[r, :], keep_theirs)
-    out = rcopy(o_mine, o_got, ex_s.at[3], ex_r.at[3], partner)
-    out.start()
-    apply(lambda r: qm[r, :], keep_mine)
-    load_wo.wait()
-    out.wait_recv()
+    apply(0, q_got)
+    apply(1, qm)
+    for copy in load_wo:
+        copy.wait()
+    for i in range(2):
+        give(i).wait_recv()
     o_all[:, theirs] = o_got[...].astype(bf16)
-
-    own_half = pl.ds(pl.multiple_of(head * 2 * N, 2 * N), 2 * N)
-    far_half = pl.ds(pl.multiple_of((1 - head) * 2 * N, 2 * N), 2 * N)
-
-    def piece(j):
-        return pl.ds(0, 2), pl.ds(pl.multiple_of(j * 32, 32), 32)
-
-    def direct(j):
-        c, r = piece(j)
-        return rcopy(gp.at[c, r], p_got.at[c, r], pt_s.at[j], pt_r.at[j], other_head)
-
-    def first_leg(j, device):
-        c, r = piece(j)
-        return rcopy(gp.at[c, r], gf1.at[c, r], rl_s.at[j], rl_r.at[j], device)
-
-    def second_leg(j, device):
-        c, r = piece(j)
-        return rcopy(gf1.at[c, r], p_got.at[c, r], pt_s.at[j], pt_r.at[j], device)
 
     @pl.loop(0, 4)
     def _(i):
         rows = pl.ds(pl.multiple_of(i * 128, 128), 128)
-        v = dot(o_all[rows, :], wo[:, far_half])
-        gp[0, rows, :] = v[:, :N]
-        gp[1, rows, :] = v[:, N:]
-
-        @pl.when(block == 0)
-        def _():
-            for j in range(4):
-                direct(i * 4 + j).start()
-
-        @pl.when(block == 1)
-        def _():
-            for j in range(2):
-                first_leg(i * 4 + 2 * j, other_block).start()
-                first_leg(i * 4 + 2 * j + 1, diagonal).start()
-
-    @pl.loop(0, 4)
-    def _(i):
-        rows = pl.ds(pl.multiple_of(i * 128, 128), 128)
-        v = dot(o_all[rows, :], wo[:, own_half])
+        v = dot(o_all[rows, :N], wo[0]) + dot(o_all[rows, N:], wo[1])
         w[0, rows, :] = v[:, :N]
         w[1, rows, :] = v[:, N:]
 
-    @pl.loop(0, 16)
-    def _(j):
-        direct(j).wait_recv()
-        _, rows = piece(j)
-        for half in range(2):
-            v = w[half, rows, :] + p_got[half, rows, :]
-            o_ref[rows, pl.ds(half * N, N)] = v.astype(bf16)
+    def add_theirs():
+        for j in range(8):
+            arrival(0, j).wait_recv()
+
+        @pl.loop(0, 4)
+        def _(i):
+            rows = pl.ds(pl.multiple_of(i * 128, 128), 128)
+            v = dot(o_far[1 - core, rows, :].astype(bf16), wo[3 - core])
+            w[0, rows, :] = w[0, rows, :] + v[:, :N]
+            w[1, rows, :] = w[1, rows, :] + v[:, N:]
+
+    def add_mine(j):
+        arrival(1, j).wait_recv()
+        rows = rows_at(j)
+        v = dot(o_far[core, rows, :].astype(bf16), wo[2 + core])
+        o_ref[rows, :N] = (w[0, rows, :] + v[:, :N]).astype(bf16)
+        o_ref[rows, N:] = (w[1, rows, :] + v[:, N:]).astype(bf16)
+
+    def relay(t, i):
+        first_leg(t, 2 * i, other_block).wait_recv()
+        second_leg(t, 2 * i, diagonal).start()
+        first_leg(t, 2 * i + 1, diagonal).wait_recv()
+        second_leg(t, 2 * i + 1, other_block).start()
 
     @pl.when(block == 0)
     def _():
-        @pl.loop(0, 16)
-        def _(j):
-            direct(j).wait_send()
+        @pl.loop(0, 4)
+        def _(i):
+            relay(0, i)
+
+        add_theirs()
+
+        @pl.loop(0, 4)
+        def _(i):
+            relay(1, i)
+            add_mine(2 * i)
+            add_mine(2 * i + 1)
+
+        for t in range(2):
+            @pl.loop(0, 8)
+            def _(j):
+                direct(t, j).wait_send()
+                second_leg(t, j, diagonal).wait_send()
+
+    @pl.when(block == 1)
+    def _():
+        add_theirs()
 
         @pl.loop(0, 8)
         def _(j):
-            first_leg(2 * j, other_block).wait_recv()
-            second_leg(2 * j, diagonal).start()
-            first_leg(2 * j + 1, diagonal).wait_recv()
-            second_leg(2 * j + 1, other_block).start()
-
-        @pl.loop(0, 16)
-        def _(j):
-            second_leg(j, diagonal).wait_send()
-
-    @pl.when(block == 1)
-    def _():
-        @pl.loop(0, 16)
-        def _(j):
-            first_leg(j, diagonal).wait_send()
-
-    for c in swaps + [out]:
+            add_mine(j)
+
+        for t in range(2):
+            @pl.loop(0, 8)
+            def _(j):
+                first_leg(t, j, diagonal).wait_send()
+
+    for c in swaps + seeds + wo_sent + [wo_swap, give(0), give(1)]:
         c.wait_send()
 
 
@@ -503,9 +598,11 @@
         in_specs=[hbm, hbm, vmem, hbm, hbm],
         out_specs=vmem,
         scratch_shapes=[
-            pltpu.VMEM((N, 4 * N), bf16), pltpu.VMEM((2 * N, 4 * N), bf16), square(3, bf16),
-            part, part, part, part, part, part, part, part, part,
+            pltpu.VMEM((N, 4 * N), bf16), pltpu.VMEM((4, N, 2 * N), bf16), square(3, bf16),
+            part, part, part, part, part, part, part, part,
             pltpu.VMEM((N, 2 * N), bf16), square(2, f32),
+            pltpu.VMEM((2, 16, 2 * N), bf16), pltpu.VMEM((2, 2, 16, N), f32),
+            square(2, f32), square(2, f32),
             tall, tall, wide, wide, tall, tall, wide, wide, pltpu.VMEM((3, 4 * N, N), bf16),
             square(3, f32), square(3, bf16), square(3, bf16), pltpu.VMEM((3, 1, N), f32),
             square(3, f32), square(3, f32), square(3, f32),
@@ -514,8 +611,10 @@
             dma((3, 2, 2, 4)), dma((3, 2, 2, 4)),
             dma((3, 2, 2, 4)), dma((3, 2, 2, 4)),
             dma((3, 2)), dma((3, 2)),
-            dma((4,)), dma((4,)),
-            dma((16,)), dma((16,)), dma((16,)), dma((16,)), dma((3,)), dma((3,)),
+            dma((6,)), dma((6,)),
+            dma((2, 16)), dma((2, 8)), dma((2, 8)), dma((2, 8)),
+            dma((2, 2)), dma((2, 2)), dma((2, 2, 2, 4)), dma((2, 2, 2, 4)),
+            dma((6,)), dma((3,)),
         ],
         compiler_params=pltpu.CompilerParams(
             collective_id=0, has_side_effects=True, vmem_limit_bytes=62 * 1024 * 1024

time: 164 us -> 158 us (0.963)
  Pallas kernels: 161 us -> 156 us
    pallas_call x1, Pallas kernels: 161 us -> 156 us  [chain(): pl.pallas_call(chain_kernel, out_shape=jax.ShapeDtypeStruct((N, 2 * N), b...]
where the time goes in v4:
time: 158 us
  Pallas kernels  156 us (99%)
  local copies, waits for them, and re-layouts  2.26 us (1%)
    pallas_call x1, Pallas kernels, chain(): pl.pallas_call(chain_kernel, out_shape=jax.ShapeDtypeStruct((N, 2 * N), b...  156 us

profile of v4, /device:TPU:8, one launch (start us, length us, event | category | flops | bytes accessed | tf_op | source)
XLA Modules:
  0.0 158.2 jit_solution(10147728628702954367)
XLA Ops:
  0.0 156.0 %shard_map.55 = bf16[512,1024]{1,0:T(8,128)(2,1)} custom-call(bf16[512,2048]{1,0:T(8,128)(2,1)} %bitcast.6, bf16[3,2048,1024]{2,1,0:T(8,128)(2,1)} %bitcast.4, bf16[2,2048]{1,0:T(2,128)(2,1)} %bitcast.7, bf16[2,3,512,512]{3,2,1,0:T(8,128)(2,1)} %w0_hbm.1, bf16[1024,2048]{1,0:T(8,128)(2,1)} %wo_hbm.1), custom_call_target="tpu_custom_call" | custom-call | tf_op jit(solution)/shard_map/pallas_call | solution.py:595
  156.0 2.3 %copy.7 = bf16[1,512,1024]{2,1,0:T(8,128)(2,1)} copy(bf16[1,512,1024]{2,1,0:T(8,128)(2,1)} %bitcast.5) | data formatting | bytes 2097152

commit v5 on v4

--- a/solution.py
+++ b/solution.py
@@ -41,8 +41,8 @@
 
 def chain_kernel(
     tok_hbm, wi_hbm, rate_ref, w0_hbm, wo_hbm, o_ref,
-    tok_v, wo, w0, ks, ys, qs, qm, k_got, y_got, q_got, o_got, o_all, o_far, seed, seed32, wog, wos,
-    kh, kl, kth, ktl, yh, yl, yth, ytl, big,
+    tok_v, wo, w0, ks, ys, qs, qm, k32, y32, q_got, o_got, o_all, o_far, seed, seed32, wog, wos,
+    kth, ktl, yth, ytl, big,
     w, wh, wl, r0, gp, gf, gf1, r1, r2,
     rs_s, rs_r, ag_s, ag_r, a1_s, a1_r, sh_s, sh_r, ex_s, ex_r,
     pt_s, pt_r, rl_s, rl_r, sd_s, sd_r, wg_s, wg_r, in_s, wi_s,
@@ -118,7 +118,9 @@
 
     swaps = [
         rcopy(src, dst, ex_s.at[n], ex_r.at[n], partner)
-        for n, (src, dst) in enumerate(((ks, k_got), (ys, y_got), (qs, q_got)))
+        for n, (src, dst) in enumerate(
+            ((ks, k32.at[pl.ds(N, N)]), (ys, y32.at[pl.ds(N, N)]), (qs, q_got))
+        )
     ]
 
     def project(n, finish):
@@ -132,14 +134,6 @@
     def rates(rows, which):
         r = jax.nn.softplus(dot_nt(tok_v[rows, :], rate_ref[...]))
         return jnp.where(which == 0, r[:, 0:1], r[:, 1:2])
-
-    def prepare(base, rows, v, h_ref, l_ref, th_ref, tl_ref):
-        hi, lo = split(v)
-        to = pl.ds(pl.multiple_of(base, 256), 256)
-        h_ref[to, :] = hi
-        l_ref[to, :] = lo
-        th_ref[:, to] = hi.T
-        tl_ref[:, to] = lo.T
 
     def put(ref, f):
         def finish(base, rows, v):
@@ -203,17 +197,9 @@
         seed32[m, n] = seed[n, :, m * N:(m + 1) * N].astype(f32)
     for copy in seeds:
         copy.start()
-    wo_sent = []
-
-    def bring_weights(m, n):
+    def bring_weights(m, n, wo_sent):
         seeds[m * 2 + n].wait_recv()
         yield from gather(wog, m, n, wg_s, wg_r, wo_sent)
-
-    bringing = [bring_weights(m, n) for m, n in SHARDS]
-
-    def bring():
-        for g in bringing:
-            next(g, None)
 
     wo_swap = rcopy(wog, wos, ex_s.at[5], ex_r.at[5], partner)
 
@@ -221,14 +207,10 @@
     project(0, put(ks, lambda r, v: normalize(v)))
     swaps[0].start()
     weights(3).start()
-    bring()
     project(1, put(ys, lambda r, v: v * rates(r, 1 - core)))
     swaps[1].start()
-    bring()
-    project(2, lambda b, r, v: prepare(b, r, normalize(v), kh, kl, kth, ktl))
-    bring()
-    project(3, lambda b, r, v: prepare(b, r, v * rates(r, core), yh, yl, yth, ytl))
-    bring()
+    project(2, put(k32, lambda r, v: normalize(v)))
+    project(3, put(y32, lambda r, v: v * rates(r, core)))
 
     def project_q():
         weights(4).start()
@@ -238,27 +220,26 @@
         project(5, put(qm, lambda r, v: normalize(v)))
 
     load_w0.wait()
-    for m in range(3):
-        start = w0[m].astype(f32)
-        w[m] = start
-        wh[m], wl[m] = split(start)
-        r0[m] = jnp.sqrt(jnp.mean(start * start, axis=0, keepdims=True))
-
-    def prepare_got(got, h_ref, l_ref, th_ref, tl_ref):
-        @pl.loop(0, 2)
-        def _(i):
-            rows = pl.ds(pl.multiple_of(i * 256, 256), 256)
-            prepare(N + i * 256, rows, got[rows, :], h_ref, l_ref, th_ref, tl_ref)
-
     swaps[0].wait_recv()
-    prepare_got(k_got, kh, kl, kth, ktl)
-    bring()
     swaps[1].wait_recv()
-    prepare_got(y_got, yh, yl, yth, ytl)
-    bring()
-    wo_swap.start()
+
+    def set_weights():
+        for m in range(3):
+            @pl.loop(0, 4)
+            def _(i):
+                rows = pl.ds(pl.multiple_of(i * 128, 128), 128)
+                w[m, rows, :] = w0[m, rows, :].astype(f32)
+
+            start = w[m]
+            r0[m] = jnp.sqrt(jnp.mean(start * start, axis=0, keepdims=True))
 
     def keep_weights():
+        wo_sent = []
+        bringing = [bring_weights(m, n, wo_sent) for m, n in SHARDS]
+        for _ in range(5):
+            for g in bringing:
+                next(g, None)
+        wo_swap.start()
         wo_swap.wait_recv()
 
         @pl.loop(0, 4)
@@ -268,6 +249,9 @@
                 columns = pl.ds(m * N, N)
                 wo[2 + core, rows, columns] = wog[m, rows, :].astype(bf16)
                 wo[3 - core, rows, columns] = wos[m, rows, :].astype(bf16)
+
+        for c in wo_sent:
+            c.wait_send()
 
     def reduce_stage(m, piece, n, got, store, i, go, ss, rs, sent):
         src = gp.at[m]
@@ -373,6 +357,7 @@
     @pl.when(block == 1)
     def _():
         project_q()
+        set_weights()
         keep_weights()
         done = []
 
@@ -388,18 +373,24 @@
     p3h, p3l = big.at[1, pl.ds(0, 2 * N)], big.at[1, pl.ds(2 * N, 2 * N)]
     p1h, p1l = big.at[2, pl.ds(0, 2 * N)], big.at[2, pl.ds(2 * N, 2 * N)]
 
-    @pl.loop(0, 4)
-    def _(i):
-        rows = pl.ds(pl.multiple_of(i * 256, 256), 256)
-        ah, al = kh[rows, :], kl[rows, :]
-        gate = mm3(ah, al, wh[0], wl[0])
-        upper = mm3(ah, al, wh[1], wl[1])
-        back = mm3(yh[rows, :], yl[rows, :], wh[2], wl[2])
-        sigma = jax.nn.sigmoid(gate)
-        active = gate * sigma
-        hh[rows, :], hl[rows, :] = split(active * upper)
-        p3h[rows, :], p3l[rows, :] = split(back * active)
-        p1h[rows, :], p1l[rows, :] = split(back * upper * sigma * (1.0 + gate * (1.0 - sigma)))
+    def forward(times):
+        @pl.loop(0, 4)
+        def _(i):
+            rows = pl.ds(pl.multiple_of(i * 256, 256), 256)
+            ah, al = split(k32[rows, :])
+            ch, cl = split(y32[rows, :])
+            gate = times(ah, al, 0)
+            upper = times(ah, al, 1)
+            back = times(ch, cl, 2)
+            kth[:, rows] = ah.T
+            ktl[:, rows] = al.T
+            yth[:, rows] = ch.T
+            ytl[:, rows] = cl.T
+            sigma = jax.nn.sigmoid(gate)
+            active = gate * sigma
+            hh[rows, :], hl[rows, :] = split(active * upper)
+            p3h[rows, :], p3l[rows, :] = split(back * active)
+            p1h[rows, :], p1l[rows, :] = split(back * upper * sigma * (1.0 + gate * (1.0 - sigma)))
 
     def product(m, lth, ltl, rh, rl):
         @pl.loop(0, 4)
@@ -422,22 +413,25 @@
         product(1, kth, ktl, p3h, p3l)
         begin(1)
         product(0, kth, ktl, p1h, p1l)
+        advance(1)
         begin(0)
+        product(2, yth, ytl, hh, hl)
         advance(1)
-        product(2, yth, ytl, hh, hl)
+        advance(0)
         begin(2)
         drive(live, finish)
 
     @pl.when(block == 0)
     def _():
         sent = []
+        forward(lambda h, l, m: dot(h, w0[m]) + dot(l, w0[m]))
         exchange(first_block, lambda m: None, sent)
         live = {m: [gather(gf, m, s, ag_s, ag_r, sent) for s in range(2)] for m in range(3)}
         for m in ORDER:
             for g in live[m]:
                 next(g)
         project_q()
-        keep_weights()
+        set_weights()
         drive(live, lambda m: update(m, gf))
         for c in sent:
             c.wait_send()
@@ -445,6 +439,7 @@
     @pl.when(block == 1)
     def _():
         sent = []
+        forward(lambda h, l, m: mm3(h, l, wh[m], wl[m]))
         exchange(last_block, lambda m: update(m, gf), sent)
         for c in sent:
             c.wait_send()
@@ -510,6 +505,11 @@
     swaps[2].wait_recv()
     apply(0, q_got)
     apply(1, qm)
+
+    @pl.when(block == 0)
+    def _():
+        keep_weights()
+
     for copy in load_wo:
         copy.wait()
     for i in range(2):
@@ -580,14 +580,13 @@
             def _(j):
                 first_leg(t, j, diagonal).wait_send()
 
-    for c in swaps + seeds + wo_sent + [wo_swap, give(0), give(1)]:
+    for c in swaps + seeds + [wo_swap, give(0), give(1)]:
         c.wait_send()
 
 
 def chain(tokens, weight, rate_weight, fast_init, output_weight):
     dma = pltpu.SemaphoreType.DMA
     square = lambda n, t: pltpu.VMEM((n, N, N), t)
-    tall = pltpu.VMEM((2 * N, N), bf16)
     wide = pltpu.VMEM((N, 2 * N), bf16)
     part = pltpu.VMEM((N, N), f32)
     vmem = pl.BlockSpec(memory_space=pltpu.VMEM)
@@ -599,11 +598,11 @@
         out_specs=vmem,
         scratch_shapes=[
             pltpu.VMEM((N, 4 * N), bf16), pltpu.VMEM((4, N, 2 * N), bf16), square(3, bf16),
-            part, part, part, part, part, part, part, part,
+            part, part, part, part, pltpu.VMEM((2 * N, N), f32), pltpu.VMEM((2 * N, N), f32), part, part,
             pltpu.VMEM((N, 2 * N), bf16), square(2, f32),
             pltpu.VMEM((2, 16, 2 * N), bf16), pltpu.VMEM((2, 2, 16, N), f32),
             square(2, f32), square(2, f32),
-            tall, tall, wide, wide, tall, tall, wide, wide, pltpu.VMEM((3, 4 * N, N), bf16),
+            wide, wide, wide, wide, pltpu.VMEM((3, 4 * N, N), bf16),
             square(3, f32), square(3, bf16), square(3, bf16), pltpu.VMEM((3, 1, N), f32),
             square(3, f32), square(3, f32), square(3, f32),
             pltpu.VMEM((3, 2, 6, 32, N), f32), pltpu.VMEM((3, 2, 6, 8, N), f32),

time: 158 us -> 149 us (0.943)
  Pallas kernels: 156 us -> 147 us
    pallas_call x1, Pallas kernels: 156 us -> 147 us  [chain(): pl.pallas_call(chain_kernel, out_shape=jax.ShapeDtypeStruct((N, 2 * N), b...]
where the time goes in v5:
time: 149 us
  Pallas kernels  147 us (99%)
  local copies, waits for them, and re-layouts  2.26 us (2%)
    pallas_call x1, Pallas kernels, chain(): pl.pallas_call(chain_kernel, out_shape=jax.ShapeDtypeStruct((N, 2 * N), b...  147 us

profile of v5, /device:TPU:8, one launch (start us, length us, event | category | flops | bytes accessed | tf_op | source)
XLA Modules:
  0.0 148.8 jit_solution(5113197001955433654)
XLA Ops:
  0.0 146.5 %shard_map.55 = bf16[512,1024]{1,0:T(8,128)(2,1)} custom-call(bf16[512,2048]{1,0:T(8,128)(2,1)} %bitcast.6, bf16[3,2048,1024]{2,1,0:T(8,128)(2,1)} %bitcast.4, bf16[2,2048]{1,0:T(2,128)(2,1)} %bitcast.7, bf16[2,3,512,512]{3,2,1,0:T(8,128)(2,1)} %w0_hbm.1, bf16[1024,2048]{1,0:T(8,128)(2,1)} %wo_hbm.1), custom_call_target="tpu_custom_call" | custom-call | tf_op jit(solution)/shard_map/pallas_call | solution.py:594
  146.5 2.3 %copy.7 = bf16[1,512,1024]{2,1,0:T(8,128)(2,1)} copy(bf16[1,512,1024]{2,1,0:T(8,128)(2,1)} %bitcast.5) | data formatting | bytes 2097152

commit v6 on v5

--- a/solution.py
+++ b/solution.py
@@ -41,7 +41,7 @@
 
 def chain_kernel(
     tok_hbm, wi_hbm, rate_ref, w0_hbm, wo_hbm, o_ref,
-    tok_v, wo, w0, ks, ys, qs, qm, k32, y32, q_got, o_got, o_all, o_far, seed, seed32, wog, wos,
+    tok_v, wo, w0, ks, ys, k32, y32, q32, u32, rate, o_got, o_all, o_far, seed, seed32, wog, wos,
     kth, ktl, yth, ytl, big,
     w, wh, wl, r0, gp, gf, gf1, r1, r2,
     rs_s, rs_r, ag_s, ag_r, a1_s, a1_r, sh_s, sh_r, ex_s, ex_r,
@@ -108,7 +108,6 @@
     )
     for device in everyone:
         pl.semaphore_signal(barrier, inc=1, device_id=device, device_id_type=MESH)
-    pl.semaphore_wait(barrier, len(everyone))
 
     def rcopy(src, dst, ss, rs, device):
         return pltpu.make_async_remote_copy(
@@ -119,27 +118,16 @@
     swaps = [
         rcopy(src, dst, ex_s.at[n], ex_r.at[n], partner)
         for n, (src, dst) in enumerate(
-            ((ks, k32.at[pl.ds(N, N)]), (ys, y32.at[pl.ds(N, N)]), (qs, q_got))
+            ((ks, k32.at[pl.ds(N, N)]), (ys, y32.at[pl.ds(N, N)]), (ks, q32.at[pl.ds(0, N)]))
         )
     ]
 
     def project(n, finish):
         weights(n).wait()
-
-        @pl.loop(0, 2)
-        def _(i):
-            rows = pl.ds(pl.multiple_of(i * 256, 256), 256)
-            finish(i * 256, rows, dot(tok_v[rows, :], big[n % 3]))
-
-    def rates(rows, which):
-        r = jax.nn.softplus(dot_nt(tok_v[rows, :], rate_ref[...]))
-        return jnp.where(which == 0, r[:, 0:1], r[:, 1:2])
-
-    def put(ref, f):
-        def finish(base, rows, v):
-            ref[rows, :] = f(rows, v)
-
-        return finish
+        return finish(dot(tok_v[...], big[n % 3]))
+
+    def chosen_rate(which):
+        return jnp.where(which == 0, rate[:, 0:1], rate[:, 1:2])
 
     def rows_of(s, j1, j2=None, off=0, count=64):
         at = s * 256 + j1 * 64 + off
@@ -191,37 +179,39 @@
         )
         for m, n in SHARDS
     ]
+    def bring_weights(m, n, wo_sent):
+        seeds[m * 2 + n].wait_recv()
+        yield from gather(wog, m, n, wg_s, wg_r, wo_sent)
+
+    wo_swap = rcopy(wog, wos, ex_s.at[5], ex_r.at[5], partner)
+
+    load_tok.wait()
+    ks[...] = project(0, normalize)
+    weights(3).start()
+    rate[...] = jax.nn.softplus(dot_nt(tok_v[...], rate_ref[...]))
+    ys[...] = project(1, lambda v: v * chosen_rate(1 - core))
+    pl.semaphore_wait(barrier, len(everyone))
+    swaps[0].start()
+    swaps[1].start()
     for copy in load_seed:
         copy.wait()
     for m, n in SHARDS:
         seed32[m, n] = seed[n, :, m * N:(m + 1) * N].astype(f32)
     for copy in seeds:
         copy.start()
-    def bring_weights(m, n, wo_sent):
-        seeds[m * 2 + n].wait_recv()
-        yield from gather(wog, m, n, wg_s, wg_r, wo_sent)
-
-    wo_swap = rcopy(wog, wos, ex_s.at[5], ex_r.at[5], partner)
-
-    load_tok.wait()
-    project(0, put(ks, lambda r, v: normalize(v)))
-    swaps[0].start()
-    weights(3).start()
-    project(1, put(ys, lambda r, v: v * rates(r, 1 - core)))
-    swaps[1].start()
-    project(2, put(k32, lambda r, v: normalize(v)))
-    project(3, put(y32, lambda r, v: v * rates(r, core)))
+    k32[:N, :] = project(2, normalize)
+    y32[:N, :] = project(3, lambda v: v * chosen_rate(core))
 
     def project_q():
         weights(4).start()
         weights(5).start()
-        project(4, put(qs, lambda r, v: normalize(v)))
+        swaps[0].wait_send()
+        ks[...] = project(4, normalize)
         swaps[2].start()
-        project(5, put(qm, lambda r, v: normalize(v)))
+        q32[N:, :] = project(5, normalize)
+        swaps[2].wait_recv()
 
     load_w0.wait()
-    swaps[0].wait_recv()
-    swaps[1].wait_recv()
 
     def set_weights():
         for m in range(3):
@@ -340,6 +330,16 @@
 
     def drive(streams, finish):
         left = {m: list(streams[m]) for m in streams}
+        work = []
+
+        def labor():
+            while work:
+                try:
+                    next(work[0])
+                    return
+                except StopIteration:
+                    work.pop(0)
+
         while left:
             for m in [m for m in ORDER if m in left]:
                 still = []
@@ -352,12 +352,84 @@
                 left[m] = still
                 if not still:
                     del left[m]
-                    finish(m)
+                    work.append(finish(m))
+                labor()
+        while work:
+            labor()
+
+    def halves(f):
+        for i in range(4):
+            f(i, pl.ds(i * 256, 256))
+            yield
+
+    def upper_of(source):
+        def one(i, rows):
+            h, l = split(source[rows, :])
+            u32[rows, :] = mm3(h, l, wh[1], wl[1])
+
+        return one
+
+    def gate_part(i):
+        return i // 2, pl.ds(i % 2 * 256, 256)
+
+    def transpose_all():
+        @pl.loop(0, 2)
+        def _(i):
+            rows = pl.ds(pl.multiple_of(i * N, N), N)
+            for source, th, tl in ((k32, kth, ktl), (y32, yth, ytl)):
+                h, l = split(source[rows, :])
+                th[:, rows] = h.T
+                tl[:, rows] = l.T
+
+    hh, hl = big.at[0, pl.ds(0, 2 * N)], big.at[0, pl.ds(2 * N, 2 * N)]
+    p3h, p3l = big.at[1, pl.ds(0, 2 * N)], big.at[1, pl.ds(2 * N, 2 * N)]
+    p1h, p1l = big.at[2, pl.ds(0, 2 * N)], big.at[2, pl.ds(2 * N, 2 * N)]
+
+    def combine(rows, gate, upper, back):
+        sigma = jax.nn.sigmoid(gate)
+        active = gate * sigma
+        hh[rows, :], hl[rows, :] = split(active * upper)
+        p3h[rows, :], p3l[rows, :] = split(back * active)
+        p1h[rows, :], p1l[rows, :] = split(back * upper * sigma * (1.0 + gate * (1.0 - sigma)))
+
+    def learned(m):
+        update(m, gf1)
+        yield
+        if m == 2:
+            def last(i, rows):
+                h, l = split(y32[rows, :])
+                combine(rows, gp[gate_part(i)], u32[rows, :], mm3(h, l, wh[2], wl[2]))
+
+            yield from halves(last)
+        elif m == 0:
+            def gate(i, rows):
+                h, l = split(k32[rows, :])
+                gp[gate_part(i)] = mm3(h, l, wh[0], wl[0])
+
+            yield from halves(gate)
+        else:
+            yield from halves(upper_of(k32))
+
+    def applied(m):
+        update(m, gf)
+        yield
+        if m == 1:
+            yield from halves(upper_of(q32))
+        if m == 0:
+            def hidden(i, rows):
+                h, l = split(q32[rows, :])
+                gate = mm3(h, l, wh[0], wl[0])
+                hh[rows, :], hl[rows, :] = split(gate * jax.nn.sigmoid(gate) * u32[rows, :])
+
+            yield from halves(hidden)
 
     @pl.when(block == 1)
     def _():
+        swaps[0].wait_recv()
+        swaps[1].wait_recv()
         project_q()
         set_weights()
+        transpose_all()
         keep_weights()
         done = []
 
@@ -365,37 +437,27 @@
             shard(m, s).wait_recv()
             yield from gather(gf1, m, s, a1_s, a1_r, done)
 
-        drive({m: [first(m, s) for s in range(2)] for m in range(3)}, lambda m: update(m, gf1))
+        drive({m: [first(m, s) for s in range(2)] for m in range(3)}, learned)
         for c in done:
             c.wait_send()
 
-    hh, hl = big.at[0, pl.ds(0, 2 * N)], big.at[0, pl.ds(2 * N, 2 * N)]
-    p3h, p3l = big.at[1, pl.ds(0, 2 * N)], big.at[1, pl.ds(2 * N, 2 * N)]
-    p1h, p1l = big.at[2, pl.ds(0, 2 * N)], big.at[2, pl.ds(2 * N, 2 * N)]
-
-    def forward(times):
-        @pl.loop(0, 4)
+    def forward(i):
+        rows = pl.ds(i * N, N)
+        ah, al = split(k32[rows, :])
+        ch, cl = split(y32[rows, :])
+        gate = dot(ah, w0[0]) + dot(al, w0[0])
+        upper = dot(ah, w0[1]) + dot(al, w0[1])
+        back = dot(ch, w0[2]) + dot(cl, w0[2])
+        kth[:, rows] = ah.T
+        ktl[:, rows] = al.T
+        yth[:, rows] = ch.T
+        ytl[:, rows] = cl.T
+        combine(rows, gate, upper, back)
+
+    def product(m, lth, ltl, rh, rl):
+        @pl.loop(0, 2)
         def _(i):
             rows = pl.ds(pl.multiple_of(i * 256, 256), 256)
-            ah, al = split(k32[rows, :])
-            ch, cl = split(y32[rows, :])
-            gate = times(ah, al, 0)
-            upper = times(ah, al, 1)
-            back = times(ch, cl, 2)
-            kth[:, rows] = ah.T
-            ktl[:, rows] = al.T
-            yth[:, rows] = ch.T
-            ytl[:, rows] = cl.T
-            sigma = jax.nn.sigmoid(gate)
-            active = gate * sigma
-            hh[rows, :], hl[rows, :] = split(active * upper)
-            p3h[rows, :], p3l[rows, :] = split(back * active)
-            p1h[rows, :], p1l[rows, :] = split(back * upper * sigma * (1.0 + gate * (1.0 - sigma)))
-
-    def product(m, lth, ltl, rh, rl):
-        @pl.loop(0, 4)
-        def _(i):
-            rows = pl.ds(pl.multiple_of(i * 128, 128), 128)
             gp[m, rows, :] = mm3(lth[rows, :], ltl[rows, :], rh[...], rl[...])
 
     def exchange(stream, finish, sent):
@@ -424,23 +486,25 @@
     @pl.when(block == 0)
     def _():
         sent = []
-        forward(lambda h, l, m: dot(h, w0[m]) + dot(l, w0[m]))
-        exchange(first_block, lambda m: None, sent)
+        forward(0)
+        swaps[0].wait_recv()
+        swaps[1].wait_recv()
+        forward(1)
+        exchange(first_block, lambda m: iter(()), sent)
         live = {m: [gather(gf, m, s, ag_s, ag_r, sent) for s in range(2)] for m in range(3)}
         for m in ORDER:
             for g in live[m]:
                 next(g)
         project_q()
         set_weights()
-        drive(live, lambda m: update(m, gf))
+        drive(live, applied)
         for c in sent:
             c.wait_send()
 
     @pl.when(block == 1)
     def _():
         sent = []
-        forward(lambda h, l, m: mm3(h, l, wh[m], wl[m]))
-        exchange(last_block, lambda m: update(m, gf), sent)
+        exchange(last_block, applied, sent)
         for c in sent:
             c.wait_send()
 
@@ -486,15 +550,12 @@
         rows = pl.ds(pl.multiple_of(i * 256, 256), 256)
         return rcopy(gp.at[0, rows], o_got.at[rows], ex_s.at[3 + i], ex_r.at[3 + i], partner)
 
-    def apply(t, q):
+    def apply(t):
         @pl.loop(0, 2)
         def _(i):
             rows = pl.ds(pl.multiple_of(i * 256, 256), 256)
-            ah, al = split(q[rows, :])
-            gate = mm3(ah, al, wh[0], wl[0])
-            upper = mm3(ah, al, wh[1], wl[1])
-            bh, bl = split(gate * jax.nn.sigmoid(gate) * upper)
-            o = normalize(mm3_nt(bh, bl, wh[2], wl[2])).astype(bf16)
+            of = pl.ds(pl.multiple_of(t * N + i * 256, 256), 256)
+            o = normalize(mm3_nt(hh[of, :], hl[of, :], wh[2], wl[2])).astype(bf16)
             gp[t, rows, :] = o.astype(f32)
             if t == 1:
                 o_all[rows, mine] = o
@@ -502,9 +563,8 @@
             if t == 0:
                 give(i).start()
 
-    swaps[2].wait_recv()
-    apply(0, q_got)
-    apply(1, qm)
+    apply(0)
+    apply(1)
 
     @pl.when(block == 0)
     def _():
@@ -516,9 +576,9 @@
         give(i).wait_recv()
     o_all[:, theirs] = o_got[...].astype(bf16)
 
-    @pl.loop(0, 4)
+    @pl.loop(0, 2)
     def _(i):
-        rows = pl.ds(pl.multiple_of(i * 128, 128), 128)
+        rows = pl.ds(pl.multiple_of(i * 256, 256), 256)
         v = dot(o_all[rows, :N], wo[0]) + dot(o_all[rows, N:], wo[1])
         w[0, rows, :] = v[:, :N]
         w[1, rows, :] = v[:, N:]
@@ -527,9 +587,9 @@
         for j in range(8):
             arrival(0, j).wait_recv()
 
-        @pl.loop(0, 4)
+        @pl.loop(0, 2)
         def _(i):
-            rows = pl.ds(pl.multiple_of(i * 128, 128), 128)
+            rows = pl.ds(pl.multiple_of(i * 256, 256), 256)
             v = dot(o_far[1 - core, rows, :].astype(bf16), wo[3 - core])
             w[0, rows, :] = w[0, rows, :] + v[:, :N]
             w[1, rows, :] = w[1, rows, :] + v[:, N:]
@@ -580,7 +640,7 @@
             def _(j):
                 first_leg(t, j, diagonal).wait_send()
 
-    for c in swaps + seeds + [wo_swap, give(0), give(1)]:
+    for c in swaps[1:] + seeds + [wo_swap, give(0), give(1)]:
         c.wait_send()
 
 
@@ -589,6 +649,7 @@
     square = lambda n, t: pltpu.VMEM((n, N, N), t)
     wide = pltpu.VMEM((N, 2 * N), bf16)
     part = pltpu.VMEM((N, N), f32)
+    tall = pltpu.VMEM((2 * N, N), f32)
     vmem = pl.BlockSpec(memory_space=pltpu.VMEM)
     hbm = pl.BlockSpec(memory_space=pl.ANY)
     return pl.pallas_call(
@@ -598,7 +659,7 @@
         out_specs=vmem,
         scratch_shapes=[
             pltpu.VMEM((N, 4 * N), bf16), pltpu.VMEM((4, N, 2 * N), bf16), square(3, bf16),
-            part, part, part, part, pltpu.VMEM((2 * N, N), f32), pltpu.VMEM((2 * N, N), f32), part, part,
+            part, part, tall, tall, tall, tall, pltpu.VMEM((N, 2), f32), part,
             pltpu.VMEM((N, 2 * N), bf16), square(2, f32),
             pltpu.VMEM((2, 16, 2 * N), bf16), pltpu.VMEM((2, 2, 16, N), f32),
             square(2, f32), square(2, f32),
@@ -616,7 +677,7 @@
             dma((6,)), dma((3,)),
         ],
         compiler_params=pltpu.CompilerParams(
-            collective_id=0, has_side_effects=True, vmem_limit_bytes=62 * 1024 * 1024
+            collective_id=0, has_side_effects=True, vmem_limit_bytes=67043328
         ),
     )(tokens, weight, rate_weight, fast_init, output_weight)
 

time: 149 us -> 159 us (1.067)
  Pallas kernels: 147 us -> 157 us
    pallas_call x1, Pallas kernels: 147 us -> 157 us  [chain(): pl.pallas_call(chain_kernel, out_shape=jax.ShapeDtypeStruct((N, 2 * N), b...]
where the time goes in v6:
time: 159 us
  Pallas kernels  157 us (99%)
  local copies, waits for them, and re-layouts  2.26 us (1%)
    pallas_call x1, Pallas kernels, chain(): pl.pallas_call(chain_kernel, out_shape=jax.ShapeDtypeStruct((N, 2 * N), b...  157 us

profile of v6, /device:TPU:8, one launch (start us, length us, event | category | flops | bytes accessed | tf_op | source)
XLA Modules:
  0.0 158.9 jit_solution(13618670177204735968)
XLA Ops:
  0.0 156.6 %shard_map.55 = bf16[512,1024]{1,0:T(8,128)(2,1)} custom-call(bf16[512,2048]{1,0:T(8,128)(2,1)} %bitcast.6, bf16[3,2048,1024]{2,1,0:T(8,128)(2,1)} %bitcast.4, bf16[2,2048]{1,0:T(2,128)(2,1)} %bitcast.7, bf16[2,3,512,512]{3,2,1,0:T(8,128)(2,1)} %w0_hbm.1, bf16[1024,2048]{1,0:T(8,128)(2,1)} %wo_hbm.1), custom_call_target="tpu_custom_call" | custom-call | tf_op jit(solution)/shard_map/pallas_call | solution.py:655
  156.6 2.3 %copy.7 = bf16[1,512,1024]{2,1,0:T(8,128)(2,1)} copy(bf16[1,512,1024]{2,1,0:T(8,128)(2,1)} %bitcast.5) | data formatting | bytes 2097152

commit v7 on v6

--- a/solution.py
+++ b/solution.py
@@ -41,7 +41,7 @@
 
 def chain_kernel(
     tok_hbm, wi_hbm, rate_ref, w0_hbm, wo_hbm, o_ref,
-    tok_v, wo, w0, ks, ys, k32, y32, q32, u32, rate, o_got, o_all, o_far, seed, seed32, wog, wos,
+    tok_v, wo, w0, ks, ys, k32, y32, q32, rate, o_got, o_all, o_far, seed, seed32, wog, wos,
     kth, ktl, yth, ytl, big,
     w, wh, wl, r0, gp, gf, gf1, r1, r2,
     rs_s, rs_r, ag_s, ag_r, a1_s, a1_r, sh_s, sh_r, ex_s, ex_r,
@@ -56,10 +56,10 @@
     z = lax.div(chip, 4)
 
     def at_x(d):
-        return {"tok": (z * 4 + lax.rem(x + d + 4, 4)) * 2 + core}
+        return {"tok": (z * 4 + lax.rem(x + d, 4)) * 2 + core}
 
     def at_z(d):
-        return {"tok": (lax.rem(z + d + 4, 4) * 4 + x) * 2 + core}
+        return {"tok": (lax.rem(z + d, 4) * 4 + x) * 2 + core}
 
     partner = {"tok": chip * 2 + (1 - core)}
     other_block = {"block": 1 - block}
@@ -103,7 +103,7 @@
 
     barrier = pltpu.get_barrier_semaphore()
     everyone = (
-        partner, at_x(1), at_x(-1), at_z(1), at_z(-1), other_block, diagonal, other_head,
+        partner, at_x(1), at_x(2), at_x(3), at_z(1), at_z(2), at_z(3), other_block, diagonal, other_head,
         {**other_block, **partner}, {**diagonal, **partner}, {**other_head, **partner},
     )
     for device in everyone:
@@ -135,9 +135,36 @@
             at = at + j2 * 16
         return pl.ds(pl.multiple_of(at, 8), count)
 
+    def reduce_direct(m, piece, n, got, store, i, go, ss, rs, sent):
+        copies = []
+        for k, d in enumerate((1, 3, 2)):
+            rows = piece(lax.rem(i + d, 4), 0, 2 * n)
+            copies.append(rcopy(gp.at[m, rows], got.at[k], ss.at[k], rs.at[k], go(d)))
+        for c in copies:
+            c.start()
+        yield
+        for c in copies:
+            c.wait_recv()
+        store(0, gp[m, piece(i, 0, 2 * n), :] + got[0] + got[1] + got[2])
+        sent.extend(copies)
+
+    def gather_direct(buf, piece, n, i, go, ss, rs, done):
+        rows = piece(i, 0, 2 * n)
+        copies = [
+            rcopy(buf.at[rows], buf.at[rows], ss.at[k], rs.at[k], go(d))
+            for k, d in enumerate((1, 3, 2))
+        ]
+        for c in copies:
+            c.start()
+        yield
+        for k, d in enumerate((1, 3, 2)):
+            rows = piece(lax.rem(i + 4 - d, 4), 0, 2 * n)
+            rcopy(buf.at[rows], buf.at[rows], ss.at[k], rs.at[k], go(d)).wait_recv()
+        done.extend(copies)
+
     def gather_stage(buf, piece, n, i, go, ss, rs, done):
         nxt, prv, far = lax.rem(i + 1, 4), lax.rem(i + 3, 4), lax.rem(i + 2, 4)
-        right, left = go(1), go(-1)
+        right, left = go(1), go(3)
 
         def send(k, rows, device):
             return rcopy(buf.at[rows], buf.at[rows], ss.at[k], rs.at[k], device)
@@ -162,7 +189,7 @@
 
     def gather(buf, m, s, ss, rs, done):
         i1, go1, i2, go2 = axes[s]
-        yield from gather_stage(
+        yield from gather_direct(
             buf.at[m], lambda j, o, c: rows_of(s, i1, j, o, c), 8, i2, go2,
             ss.at[m, s, 0], rs.at[m, s, 0], done,
         )
@@ -246,7 +273,7 @@
     def reduce_stage(m, piece, n, got, store, i, go, ss, rs, sent):
         src = gp.at[m]
         nxt, prv, far = lax.rem(i + 1, 4), lax.rem(i + 3, 4), lax.rem(i + 2, 4)
-        right, left = go(1), go(-1)
+        right, left = go(1), go(3)
         c0 = rcopy(src.at[piece(far, 0, n)], got.at[0], ss.at[0], rs.at[0], right)
         c1 = rcopy(src.at[piece(far, n, n)], got.at[1], ss.at[1], rs.at[1], left)
         c2 = rcopy(src.at[piece(nxt, n, n)], got.at[2], ss.at[2], rs.at[2], right)
@@ -278,16 +305,16 @@
         i1, go1, i2, go2 = axes[s]
 
         def store1(o, v):
-            gp[m, rows_of(s, i1, None, o, 32), :] = v
+            gp[m, rows_of(s, i1, None, o, v.shape[0]), :] = v
 
         def store2(o, v):
-            gf[m, rows_of(s, i1, i2, o, 8), :] = v
+            gf[m, rows_of(s, i1, i2, o, 16), :] = v
 
         yield from reduce_stage(
             m, lambda j, o, c: rows_of(s, j, None, o, c), 32, r1.at[m, s], store1, i1, go1,
             rs_s.at[m, s, 0], rs_r.at[m, s, 0], sent,
         )
-        yield from reduce_stage(
+        yield from reduce_direct(
             m, lambda j, o, c: rows_of(s, i1, j, o, c), 8, r2.at[m, s], store2, i2, go2,
             rs_s.at[m, s, 1], rs_r.at[m, s, 1], sent,
         )
@@ -330,16 +357,6 @@
 
     def drive(streams, finish):
         left = {m: list(streams[m]) for m in streams}
-        work = []
-
-        def labor():
-            while work:
-                try:
-                    next(work[0])
-                    return
-                except StopIteration:
-                    work.pop(0)
-
         while left:
             for m in [m for m in ORDER if m in left]:
                 still = []
@@ -352,25 +369,7 @@
                 left[m] = still
                 if not still:
                     del left[m]
-                    work.append(finish(m))
-                labor()
-        while work:
-            labor()
-
-    def halves(f):
-        for i in range(4):
-            f(i, pl.ds(i * 256, 256))
-            yield
-
-    def upper_of(source):
-        def one(i, rows):
-            h, l = split(source[rows, :])
-            u32[rows, :] = mm3(h, l, wh[1], wl[1])
-
-        return one
-
-    def gate_part(i):
-        return i // 2, pl.ds(i % 2 * 256, 256)
+                    finish(m)
 
     def transpose_all():
         @pl.loop(0, 2)
@@ -392,36 +391,15 @@
         p3h[rows, :], p3l[rows, :] = split(back * active)
         p1h[rows, :], p1l[rows, :] = split(back * upper * sigma * (1.0 + gate * (1.0 - sigma)))
 
-    def learned(m):
-        update(m, gf1)
-        yield
-        if m == 2:
-            def last(i, rows):
-                h, l = split(y32[rows, :])
-                combine(rows, gp[gate_part(i)], u32[rows, :], mm3(h, l, wh[2], wl[2]))
-
-            yield from halves(last)
-        elif m == 0:
-            def gate(i, rows):
-                h, l = split(k32[rows, :])
-                gp[gate_part(i)] = mm3(h, l, wh[0], wl[0])
-
-            yield from halves(gate)
-        else:
-            yield from halves(upper_of(k32))
-
-    def applied(m):
-        update(m, gf)
-        yield
-        if m == 1:
-            yield from halves(upper_of(q32))
-        if m == 0:
-            def hidden(i, rows):
-                h, l = split(q32[rows, :])
-                gate = mm3(h, l, wh[0], wl[0])
-                hh[rows, :], hl[rows, :] = split(gate * jax.nn.sigmoid(gate) * u32[rows, :])
-
-            yield from halves(hidden)
+    def learn():
+        @pl.loop(0, 2)
+        def _(i):
+            rows = pl.ds(pl.multiple_of(i * N, N), N)
+            ah, al = split(k32[rows, :])
+            ch, cl = split(y32[rows, :])
+            gate = mm3(ah, al, wh[0], wl[0])
+            upper = mm3(ah, al, wh[1], wl[1])
+            combine(rows, gate, upper, mm3(ch, cl, wh[2], wl[2]))
 
     @pl.when(block == 1)
     def _():
@@ -437,7 +415,8 @@
             shard(m, s).wait_recv()
             yield from gather(gf1, m, s, a1_s, a1_r, done)
 
-        drive({m: [first(m, s) for s in range(2)] for m in range(3)}, learned)
+        drive({m: [first(m, s) for s in range(2)] for m in range(3)}, lambda m: update(m, gf1))
+        learn()
         for c in done:
             c.wait_send()
 
@@ -468,18 +447,11 @@
             for g in live[m]:
                 next(g)
 
-        def advance(m):
-            for g in live[m]:
-                next(g)
-
         product(1, kth, ktl, p3h, p3l)
         begin(1)
         product(0, kth, ktl, p1h, p1l)
-        advance(1)
         begin(0)
         product(2, yth, ytl, hh, hl)
-        advance(1)
-        advance(0)
         begin(2)
         drive(live, finish)
 
@@ -490,26 +462,29 @@
         swaps[0].wait_recv()
         swaps[1].wait_recv()
         forward(1)
-        exchange(first_block, lambda m: iter(()), sent)
+        exchange(first_block, lambda m: None, sent)
         live = {m: [gather(gf, m, s, ag_s, ag_r, sent) for s in range(2)] for m in range(3)}
         for m in ORDER:
             for g in live[m]:
                 next(g)
         project_q()
         set_weights()
-        drive(live, applied)
+        drive(live, lambda m: update(m, gf))
         for c in sent:
             c.wait_send()
 
     @pl.when(block == 1)
     def _():
         sent = []
-        exchange(last_block, applied, sent)
+        exchange(last_block, lambda m: update(m, gf), sent)
         for c in sent:
             c.wait_send()
 
     def rows_at(j):
         return pl.ds(pl.multiple_of(j * 64, 64), 64)
+
+    WAYS = (other_block, diagonal, other_block, diagonal)
+    WAYS_ON = (diagonal, other_block, diagonal, other_block)
 
     receivers = ({"tok": partner["tok"]}, {})
 
@@ -542,9 +517,8 @@
 
         @pl.when(block == 1)
         def _():
-            for j in range(0, 4, 2):
-                first_leg(t, i * 4 + j, other_block).start()
-                first_leg(t, i * 4 + j + 1, diagonal).start()
+            for j in range(4):
+                first_leg(t, i * 4 + j, WAYS[j]).start()
 
     def give(i):
         rows = pl.ds(pl.multiple_of(i * 256, 256), 256)
@@ -554,8 +528,11 @@
         @pl.loop(0, 2)
         def _(i):
             rows = pl.ds(pl.multiple_of(i * 256, 256), 256)
-            of = pl.ds(pl.multiple_of(t * N + i * 256, 256), 256)
-            o = normalize(mm3_nt(hh[of, :], hl[of, :], wh[2], wl[2])).astype(bf16)
+            ah, al = split(q32[pl.ds(pl.multiple_of(t * N + i * 256, 256), 256), :])
+            gate = mm3(ah, al, wh[0], wl[0])
+            upper = mm3(ah, al, wh[1], wl[1])
+            bh, bl = split(gate * jax.nn.sigmoid(gate) * upper)
+            o = normalize(mm3_nt(bh, bl, wh[2], wl[2])).astype(bf16)
             gp[t, rows, :] = o.astype(f32)
             if t == 1:
                 o_all[rows, mine] = o
@@ -602,24 +579,23 @@
         o_ref[rows, N:] = (w[1, rows, :] + v[:, N:]).astype(bf16)
 
     def relay(t, i):
-        first_leg(t, 2 * i, other_block).wait_recv()
-        second_leg(t, 2 * i, diagonal).start()
-        first_leg(t, 2 * i + 1, diagonal).wait_recv()
-        second_leg(t, 2 * i + 1, other_block).start()
+        for j in range(4):
+            first_leg(t, 4 * i + j, WAYS[j]).wait_recv()
+            second_leg(t, 4 * i + j, WAYS_ON[j]).start()
 
     @pl.when(block == 0)
     def _():
-        @pl.loop(0, 4)
+        @pl.loop(0, 2)
         def _(i):
             relay(0, i)
 
         add_theirs()
 
-        @pl.loop(0, 4)
+        @pl.loop(0, 2)
         def _(i):
             relay(1, i)
-            add_mine(2 * i)
-            add_mine(2 * i + 1)
+            for j in range(4):
+                add_mine(4 * i + j)
 
         for t in range(2):
             @pl.loop(0, 8)
@@ -659,14 +635,14 @@
         out_specs=vmem,
         scratch_shapes=[
             pltpu.VMEM((N, 4 * N), bf16), pltpu.VMEM((4, N, 2 * N), bf16), square(3, bf16),
-            part, part, tall, tall, tall, tall, pltpu.VMEM((N, 2), f32), part,
+            part, part, tall, tall, tall, pltpu.VMEM((N, 2), f32), part,
             pltpu.VMEM((N, 2 * N), bf16), square(2, f32),
             pltpu.VMEM((2, 16, 2 * N), bf16), pltpu.VMEM((2, 2, 16, N), f32),
             square(2, f32), square(2, f32),
             wide, wide, wide, wide, pltpu.VMEM((3, 4 * N, N), bf16),
             square(3, f32), square(3, bf16), square(3, bf16), pltpu.VMEM((3, 1, N), f32),
             square(3, f32), square(3, f32), square(3, f32),
-            pltpu.VMEM((3, 2, 6, 32, N), f32), pltpu.VMEM((3, 2, 6, 8, N), f32),
+            pltpu.VMEM((3, 2, 6, 32, N), f32), pltpu.VMEM((3, 2, 3, 16, N), f32),
             dma((3, 2, 2, 6)), dma((3, 2, 2, 6)),
             dma((3, 2, 2, 4)), dma((3, 2, 2, 4)),
             dma((3, 2, 2, 4)), dma((3, 2, 2, 4)),

time: 159 us -> 147 us (0.925)
  Pallas kernels: 157 us -> 145 us
    pallas_call x1, Pallas kernels: 157 us -> 145 us  [chain(): pl.pallas_call(chain_kernel, out_shape=jax.ShapeDtypeStruct((N, 2 * N), b...]
where the time goes in v7:
time: 147 us
  Pallas kernels  145 us (99%)
  local copies, waits for them, and re-layouts  2.26 us (2%)
    pallas_call x1, Pallas kernels, chain(): pl.pallas_call(chain_kernel, out_shape=jax.ShapeDtypeStruct((N, 2 * N), b...  145 us

profile of v7, /device:TPU:8, one launch (start us, length us, event | category | flops | bytes accessed | tf_op | source)
XLA Modules:
  0.0 147.0 jit_solution(9194423219433597705)
XLA Ops:
  0.0 144.7 %shard_map.55 = bf16[512,1024]{1,0:T(8,128)(2,1)} custom-call(bf16[512,2048]{1,0:T(8,128)(2,1)} %bitcast.6, bf16[3,2048,1024]{2,1,0:T(8,128)(2,1)} %bitcast.4, bf16[2,2048]{1,0:T(2,128)(2,1)} %bitcast.7, bf16[2,3,512,512]{3,2,1,0:T(8,128)(2,1)} %w0_hbm.1, bf16[1024,2048]{1,0:T(8,128)(2,1)} %wo_hbm.1), custom_call_target="tpu_custom_call" | custom-call | tf_op jit(solution)/shard_map/pallas_call | solution.py:631
  144.7 2.3 %copy.7 = bf16[1,512,1024]{2,1,0:T(8,128)(2,1)} copy(bf16[1,512,1024]{2,1,0:T(8,128)(2,1)} %bitcast.5) | data formatting | bytes 2097152

commit v8 on v7

--- a/solution.py
+++ b/solution.py
@@ -236,7 +236,6 @@
         ks[...] = project(4, normalize)
         swaps[2].start()
         q32[N:, :] = project(5, normalize)
-        swaps[2].wait_recv()
 
     load_w0.wait()
 
@@ -540,6 +539,7 @@
             if t == 0:
                 give(i).start()
 
+    swaps[2].wait_recv()
     apply(0)
     apply(1)
 

time: 147 us -> 147 us (level)
  no operation moved by 1% of the time
where the time goes in v8:
time: 147 us
  Pallas kernels  145 us (99%)
  local copies, waits for them, and re-layouts  2.26 us (2%)
    pallas_call x1, Pallas kernels, chain(): pl.pallas_call(chain_kernel, out_shape=jax.ShapeDtypeStruct((N, 2 * N), b...  145 us

profile of v8, /device:TPU:8, one launch (start us, length us, event | category | flops | bytes accessed | tf_op | source)
XLA Modules:
  0.0 146.8 jit_solution(17189769539175584082)
XLA Ops:
  0.0 144.5 %shard_map.55 = bf16[512,1024]{1,0:T(8,128)(2,1)} custom-call(bf16[512,2048]{1,0:T(8,128)(2,1)} %bitcast.6, bf16[3,2048,1024]{2,1,0:T(8,128)(2,1)} %bitcast.4, bf16[2,2048]{1,0:T(2,128)(2,1)} %bitcast.7, bf16[2,3,512,512]{3,2,1,0:T(8,128)(2,1)} %w0_hbm.1, bf16[1024,2048]{1,0:T(8,128)(2,1)} %wo_hbm.1), custom_call_target="tpu_custom_call" | custom-call | tf_op jit(solution)/shard_map/pallas_call | solution.py:631
  144.5 2.3 %copy.7 = bf16[1,512,1024]{2,1,0:T(8,128)(2,1)} copy(bf16[1,512,1024]{2,1,0:T(8,128)(2,1)} %bitcast.5) | data formatting | bytes 2097152

commit v9 on v8

--- a/solution.py
+++ b/solution.py
@@ -589,13 +589,15 @@
         def _(i):
             relay(0, i)
 
+        @pl.loop(0, 2)
+        def _(i):
+            relay(1, i)
+
         add_theirs()
 
-        @pl.loop(0, 2)
-        def _(i):
-            relay(1, i)
-            for j in range(4):
-                add_mine(4 * i + j)
+        @pl.loop(0, 8)
+        def _(j):
+            add_mine(j)
 
         for t in range(2):
             @pl.loop(0, 8)

time: 147 us -> 147 us (level)
  no operation moved by 1% of the time
where the time goes in v9:
time: 147 us
  Pallas kernels  145 us (99%)
  local copies, waits for them, and re-layouts  2.26 us (2%)
    pallas_call x1, Pallas kernels, chain(): pl.pallas_call(chain_kernel, out_shape=jax.ShapeDtypeStruct((N, 2 * N), b...  145 us

profile of v9, /device:TPU:8, one launch (start us, length us, event | category | flops | bytes accessed | tf_op | source)
XLA Modules:
  0.0 146.8 jit_solution(5017366508183209046)
XLA Ops:
  0.0 144.5 %shard_map.55 = bf16[512,1024]{1,0:T(8,128)(2,1)} custom-call(bf16[512,2048]{1,0:T(8,128)(2,1)} %bitcast.6, bf16[3,2048,1024]{2,1,0:T(8,128)(2,1)} %bitcast.4, bf16[2,2048]{1,0:T(2,128)(2,1)} %bitcast.7, bf16[2,3,512,512]{3,2,1,0:T(8,128)(2,1)} %w0_hbm.1, bf16[1024,2048]{1,0:T(8,128)(2,1)} %wo_hbm.1), custom_call_target="tpu_custom_call" | custom-call | tf_op jit(solution)/shard_map/pallas_call | solution.py:633
  144.5 2.3 %copy.7 = bf16[1,512,1024]{2,1,0:T(8,128)(2,1)} copy(bf16[1,512,1024]{2,1,0:T(8,128)(2,1)} %bitcast.5) | data formatting | bytes 2097152
